TPU v7x, 32 devices: a whole 2x2x4 slice. The times are simulated.
32 devices in a mesh: seq: 8 (over y, x, core), str: 4 (over z).
Axes of the slice: x: 2, y: 2, z: 4, core: 2. Of those that a mesh axis runs over, the one named last changes fastest.
Arguments:
- hidden: bfloat16 [4, 2048, 960], P('str', 'seq'), may hold values from -6 to 6
- lengths: int32 [4, 5], P('str'), may hold values from 1 to 768, 2048 in all within a row
- depth: int32 [4, 2048], P('str', 'seq'), may hold values from 1 to 3
- cotangent: float32 [4, 2048, 960], P('str', 'seq'), may hold values from -6 to 6
- norm1_gain: float32 [960], replicated, may hold values from 0.5 to 1.5
- w_query: bfloat16 [960, 960], replicated, may hold values from -0.1875 to 0.1875
- w_key: bfloat16 [960, 320], replicated, may hold values from -0.1875 to 0.1875
- w_value: bfloat16 [960, 320], replicated, may hold values from -0.1875 to 0.1875
- w_out: bfloat16 [960, 960], replicated, may hold values from -0.5 to 0.5
- norm2_gain: float32 [960], replicated, may hold values from 0.5 to 1.5
- w_gate: bfloat16 [960, 2560], replicated, may hold values from -0.1875 to 0.1875
- w_up: bfloat16 [960, 2560], replicated, may hold values from -0.1875 to 0.1875
- w_down: bfloat16 [2560, 960], replicated, may hold values from -0.125 to 0.125
- router: bfloat16 [3, 960], replicated, may hold values from -0.1875 to 0.1875
Outputs:
- mixed: bfloat16 [4, 2048, 960], P('str', 'seq')
- grad_hidden: float32 [4, 2048, 960], P('str', 'seq')
- grad_norm1_gain: float32 [960], P('str')
- grad_w_query: float32 [960, 960], P('str')
- grad_w_key: float32 [960, 320], P('str')
- grad_w_value: float32 [960, 320], P('str')
- grad_w_out: float32 [960, 960], P('str')
- grad_norm2_gain: float32 [960], P('str')
- grad_w_gate: float32 [960, 2560], P('str')
- grad_w_up: float32 [960, 2560], P('str')
- grad_w_down: float32 [2560, 960], P('str')
- grad_router: float32 [3, 960], P(None, 'str')
Inputs may be any that keep to these rules, and one draw needn't show every extreme that they name: `lengths`: each row sums to 2048 and holds one entry of exactly 768.
All inputs are finite; a program needn't handle non-finite values.
Results may differ from a plain program's by a relative error of at most 0.025.
Values may be sent and summed in bfloat16 or wider, within the bound.
No kernel may reach another device: no remote copies, remote signals or barrier semaphores. Data moves between devices by JAX's collectives and lax.ppermute only.
A program may use at most 192 MiB of HBM per device.

v0:
```python
import math

import jax
import jax.numpy as jnp
from jax import lax
from jax.sharding import PartitionSpec as P

HD = 64
R = 3
REACH = 3


EPSILON = 1e-05


def shifted(block, axis, distance):
    devices = range(lax.axis_size(axis))
    route = [(i - distance, i) for i in devices if i - distance in devices]
    return lax.ppermute(block, axis, route)


def rms_forward(values, gain):
    inverse = lax.rsqrt(jnp.mean(values * values, axis=-1, keepdims=True) + EPSILON)
    return (values * inverse * gain, inverse)


def rms_backward(values, inverse, gain, grad_out):
    scaled = grad_out * gain
    grad_gain = jnp.sum(grad_out * values * inverse, axis=0)
    grad_in = inverse * scaled - values * inverse * inverse * inverse * jnp.mean(
        scaled * values, axis=-1, keepdims=True
    )
    return (grad_in, grad_gain)


def rotate(values, cosine_tab, sine_tab):
    half = values.shape[-1] // 2
    first = values[..., :half]
    second = values[..., half:]
    return jnp.concatenate(
        [first * cosine_tab - second * sine_tab, second * cosine_tab + first * sine_tab], -1
    )


def unrotate(grads, cosine_tab, sine_tab):
    half = grads.shape[-1] // 2
    first = grads[..., :half]
    second = grads[..., half:]
    return jnp.concatenate(
        [first * cosine_tab + second * sine_tab, second * cosine_tab - first * sine_tab], -1
    )


def doc_tables(positions, doc_lengths):
    ends = jnp.cumsum(doc_lengths, dtype=jnp.int32)
    after = positions[:, None] >= ends[None, :]
    doc_index = jnp.sum(after.astype(jnp.int32), axis=1, dtype=jnp.int32)
    offset = jnp.sum(jnp.where(after, doc_lengths[None, :], 0), axis=1, dtype=jnp.int32)
    return (doc_index, positions - offset)


def head_scores(query_grp, key_grp, allowed):
    scores = jnp.einsum(
        "qgd,td->gqt", query_grp, key_grp, preferred_element_type=jnp.float32
    ) * HD ** (-0.5)
    return jnp.where(allowed[None], scores, -1e30)


def attend_head(query_grp, key_grp, value_grp, allowed):
    scores = head_scores(query_grp, key_grp, allowed)
    peak = jnp.max(scores, axis=-1, keepdims=True)
    weights = jnp.exp(scores - peak)
    total = jnp.sum(weights, axis=-1, keepdims=True)
    probs = (weights / total).astype(jnp.bfloat16)
    output = jnp.einsum("gqt,td->qgd", probs, value_grp, preferred_element_type=jnp.float32)
    return (output, peak[..., 0] + jnp.log(total[..., 0]))


def attend_back(query_grp, key_grp, value_grp, allowed, log_total, grad_out):
    scores = head_scores(query_grp, key_grp, allowed)
    probs_full = jnp.exp(scores - log_total[..., None])
    probs = probs_full.astype(jnp.bfloat16)
    grad_probs = jnp.einsum("qgd,td->gqt", grad_out, value_grp, preferred_element_type=jnp.float32)
    grad_value = jnp.einsum("gqt,qgd->td", probs, grad_out, preferred_element_type=jnp.float32)
    delta = jnp.sum(probs_full * grad_probs, axis=-1, keepdims=True)
    grad_scores = (probs_full * (grad_probs - delta)).astype(jnp.bfloat16)
    grad_query = jnp.einsum(
        "gqt,td->qgd", grad_scores, key_grp, preferred_element_type=jnp.float32
    ) * HD ** (-0.5)
    grad_key = jnp.einsum(
        "gqt,qgd->td", grad_scores, query_grp, preferred_element_type=jnp.float32
    ) * HD ** (-0.5)
    return (grad_query, grad_key, grad_value)


def stack_heads(queries, keys_all, values_all):
    rows = queries.shape[0]
    kv_heads = keys_all.shape[1] // HD
    query_stack = queries.reshape(rows, kv_heads, -1, HD).transpose(1, 0, 2, 3)
    key_stack = keys_all.reshape(-1, kv_heads, HD).transpose(1, 0, 2)
    value_stack = values_all.reshape(-1, kv_heads, HD).transpose(1, 0, 2)
    return (query_stack, key_stack, value_stack)


def attention_forward(queries, keys_all, values_all, allowed):
    rows = queries.shape[0]
    stacks = stack_heads(queries, keys_all, values_all)
    outputs, log_total = lax.map(
        lambda group: attend_head(group[0], group[1], group[2], allowed), stacks
    )
    return (outputs.transpose(1, 0, 2, 3).reshape(rows, -1), log_total)


def attention_backward(queries, keys_all, values_all, allowed, log_total, grad_out):
    rows = queries.shape[0]
    kv_heads = keys_all.shape[1] // HD
    query_stack, key_stack, value_stack = stack_heads(queries, keys_all, values_all)
    grad_stack = grad_out.reshape(rows, kv_heads, -1, HD).transpose(1, 0, 2, 3)
    grad_query, grad_key, grad_value = lax.map(
        lambda group: attend_back(group[0], group[1], group[2], allowed, group[3], group[4]),
        (query_stack, key_stack, value_stack, log_total, grad_stack),
    )
    grad_query = grad_query.transpose(1, 0, 2, 3).reshape(rows, -1)
    grad_key = grad_key.transpose(1, 0, 2).reshape(-1, keys_all.shape[1])
    grad_value = grad_value.transpose(1, 0, 2).reshape(-1, keys_all.shape[1])
    return (grad_query, grad_key, grad_value)


def fetch_prior(payload):
    received = [
        shifted((payload[0], payload[1], payload[2]), "seq", distance)
        for distance in range(REACH, 0, -1)
    ]
    keys_all = jnp.concatenate([item[0] for item in received] + [payload[0]], 0)
    values_all = jnp.concatenate([item[1] for item in received] + [payload[1]], 0)
    flags_all = jnp.concatenate([item[2] for item in received] + [payload[2]], 0)
    return (keys_all, values_all, flags_all)


def return_prior(grad_keys, grad_values, rows):
    local_keys = grad_keys[REACH * rows :]
    local_values = grad_values[REACH * rows :]
    for distance in range(1, REACH + 1):
        start = (REACH - distance) * rows
        moved = (
            shifted(grad_keys[start : start + rows].astype(jnp.bfloat16), "seq", -distance).astype(
                jnp.float32
            ),
            shifted(
                grad_values[start : start + rows].astype(jnp.bfloat16), "seq", -distance
            ).astype(jnp.float32),
        )
        local_keys = local_keys + moved[0]
        local_values = local_values + moved[1]
    return (local_keys, local_values)


def share_grads(grads):
    shares = (
        lax.psum_scatter(
            grads[0].astype(jnp.bfloat16), "str", scatter_dimension=0, tiled=True
        ).astype(jnp.float32),
        lax.psum_scatter(
            grads[1].astype(jnp.bfloat16), "str", scatter_dimension=0, tiled=True
        ).astype(jnp.float32),
        lax.psum_scatter(
            grads[2].astype(jnp.bfloat16), "str", scatter_dimension=0, tiled=True
        ).astype(jnp.float32),
        lax.psum_scatter(
            grads[3].astype(jnp.bfloat16), "str", scatter_dimension=0, tiled=True
        ).astype(jnp.float32),
        lax.psum_scatter(
            grads[4].astype(jnp.bfloat16), "str", scatter_dimension=0, tiled=True
        ).astype(jnp.float32),
        lax.psum_scatter(
            grads[5].astype(jnp.bfloat16), "str", scatter_dimension=0, tiled=True
        ).astype(jnp.float32),
        lax.psum_scatter(
            grads[6].astype(jnp.bfloat16), "str", scatter_dimension=0, tiled=True
        ).astype(jnp.float32),
        lax.psum_scatter(
            grads[7].astype(jnp.bfloat16), "str", scatter_dimension=0, tiled=True
        ).astype(jnp.float32),
        lax.psum_scatter(
            grads[8].astype(jnp.bfloat16), "str", scatter_dimension=0, tiled=True
        ).astype(jnp.float32),
        lax.psum_scatter(
            grads[9].astype(jnp.bfloat16), "str", scatter_dimension=1, tiled=True
        ).astype(jnp.float32),
    )
    return (
        lax.psum(shares[0].astype(jnp.bfloat16), "seq").astype(jnp.float32),
        lax.psum(shares[1].astype(jnp.bfloat16), "seq").astype(jnp.float32),
        lax.psum(shares[2].astype(jnp.bfloat16), "seq").astype(jnp.float32),
        lax.psum(shares[3].astype(jnp.bfloat16), "seq").astype(jnp.float32),
        lax.psum(shares[4].astype(jnp.bfloat16), "seq").astype(jnp.float32),
        lax.psum(shares[5].astype(jnp.bfloat16), "seq").astype(jnp.float32),
        lax.psum(shares[6].astype(jnp.bfloat16), "seq").astype(jnp.float32),
        lax.psum(shares[7].astype(jnp.bfloat16), "seq").astype(jnp.float32),
        lax.psum(shares[8].astype(jnp.bfloat16), "seq").astype(jnp.float32),
        lax.psum(shares[9].astype(jnp.bfloat16), "seq").astype(jnp.float32),
    )


def per_device(
    hidden,
    lengths,
    depth,
    cotangent,
    norm1_gain,
    w_query,
    w_key,
    w_value,
    w_out,
    norm2_gain,
    w_gate,
    w_up,
    w_down,
    router,
):
    rows = hidden.shape[1]
    seq_index = lax.axis_index("seq")
    local_pos = seq_index * rows + jnp.arange(rows, dtype=jnp.int32)
    key_pos = (seq_index - REACH) * rows + jnp.arange((REACH + 1) * rows, dtype=jnp.int32)
    doc_lengths = lengths[0]
    query_doc, place = doc_tables(local_pos, doc_lengths)
    key_doc, unused_place = doc_tables(key_pos, doc_lengths)
    base_mask = (
        (key_pos[None, :] >= 0)
        & (key_pos[None, :] <= local_pos[:, None])
        & (key_doc[None, :] == query_doc[:, None])
    )
    own_key = key_pos[None, :] == local_pos[:, None]
    half = HD // 2
    freqs = jnp.exp(-math.log(10000.0) * 2.0 * jnp.arange(half, dtype=jnp.float32) / HD)
    angles = place.astype(jnp.float32)[:, None, None] * freqs[None, None, :]
    cosine_tab = jnp.cos(angles)
    sine_tab = jnp.sin(angles)
    depth_row = depth[0]
    router_rows = router.astype(jnp.float32)

    def project(state):
        normed, inverse1 = rms_forward(state, norm1_gain)
        normed_low = normed.astype(jnp.bfloat16)
        query_pre = jnp.dot(normed_low, w_query, preferred_element_type=jnp.float32)
        key_pre = jnp.dot(normed_low, w_key, preferred_element_type=jnp.float32)
        value_pre = jnp.dot(normed_low, w_value, preferred_element_type=jnp.float32)
        query_low = (
            rotate(query_pre.reshape(rows, -1, HD), cosine_tab, sine_tab)
            .reshape(rows, -1)
            .astype(jnp.bfloat16)
        )
        key_low = (
            rotate(key_pre.reshape(rows, -1, HD), cosine_tab, sine_tab)
            .reshape(rows, -1)
            .astype(jnp.bfloat16)
        )
        return (inverse1, normed_low, query_low, key_low, value_pre.astype(jnp.bfloat16))

    def branches(state, attended_low, level):
        attn_out = jnp.dot(attended_low, w_out, preferred_element_type=jnp.float32)
        mid_state = state + attn_out
        normed2, inverse2 = rms_forward(mid_state, norm2_gain)
        normed2_low = normed2.astype(jnp.bfloat16)
        gate_pre = jnp.dot(normed2_low, w_gate, preferred_element_type=jnp.float32)
        up_pre = jnp.dot(normed2_low, w_up, preferred_element_type=jnp.float32)
        hidden_act = (jax.nn.silu(gate_pre) * up_pre).astype(jnp.bfloat16)
        ffn_out = jnp.dot(hidden_act, w_down, preferred_element_type=jnp.float32)
        gate_prob = jax.nn.sigmoid(
            jnp.dot(state, router_rows[level], precision=lax.Precision.HIGHEST)
        )
        active = (depth_row > level).astype(jnp.float32)
        return (
            attn_out,
            mid_state,
            inverse2,
            normed2_low,
            gate_pre,
            up_pre,
            hidden_act,
            ffn_out,
            gate_prob,
            active,
        )

    state = hidden[0].astype(jnp.float32)
    saved = []
    for level in range(R):
        inverse1, normed_low, query_low, key_low, value_low = project(state)
        flags = (depth_row > level).astype(jnp.int32)
        keys_all, values_all, flags_all = fetch_prior((key_low, value_low, flags))
        allowed = base_mask & ((flags_all > 0)[None, :] | own_key)
        attended, log_total = attention_forward(query_low, keys_all, values_all, allowed)
        attended_low = attended.astype(jnp.bfloat16)
        (
            attn_out,
            mid_state,
            inverse2,
            normed2_low,
            gate_pre,
            up_pre,
            hidden_act,
            ffn_out,
            gate_prob,
            active,
        ) = branches(state, attended_low, level)
        saved.append((state, keys_all, values_all, allowed, log_total, attended_low))
        state = state + (active * gate_prob)[:, None] * (attn_out + ffn_out)
    mixed = state.astype(jnp.bfloat16)[None]
    grad_state = cotangent[0]
    summed = None
    for level in range(R - 1, -1, -1):
        state, keys_all, values_all, allowed, log_total, attended_low = saved[level]
        inverse1, normed_low, query_low, key_low, value_low = project(state)
        (
            attn_out,
            mid_state,
            inverse2,
            normed2_low,
            gate_pre,
            up_pre,
            hidden_act,
            ffn_out,
            gate_prob,
            active,
        ) = branches(state, attended_low, level)
        both = attn_out + ffn_out
        grad_branch = (active * gate_prob)[:, None] * grad_state
        grad_logit = jnp.sum(grad_state * both, axis=-1) * active * gate_prob * (1.0 - gate_prob)
        grad_router_row = jnp.dot(grad_logit, state, precision=lax.Precision.HIGHEST)
        grad_next = grad_state + grad_logit[:, None] * router_rows[level][None, :]
        grad_ffn = grad_branch.astype(jnp.bfloat16)
        grad_down = jnp.einsum(
            "tf,td->fd", hidden_act, grad_ffn, preferred_element_type=jnp.float32
        )
        grad_act = jnp.einsum("td,fd->tf", grad_ffn, w_down, preferred_element_type=jnp.float32)
        sigma = jax.nn.sigmoid(gate_pre)
        grad_gate = (grad_act * up_pre * sigma * (1.0 + gate_pre * (1.0 - sigma))).astype(
            jnp.bfloat16
        )
        grad_up_pre = (grad_act * gate_pre * sigma).astype(jnp.bfloat16)
        grad_gate_w = jnp.einsum(
            "td,tf->df", normed2_low, grad_gate, preferred_element_type=jnp.float32
        )
        grad_up_w = jnp.einsum(
            "td,tf->df", normed2_low, grad_up_pre, preferred_element_type=jnp.float32
        )
        grad_normed2 = jnp.einsum(
            "tf,df->td", grad_gate, w_gate, preferred_element_type=jnp.float32
        )
        grad_normed2 = grad_normed2 + jnp.einsum(
            "tf,df->td", grad_up_pre, w_up, preferred_element_type=jnp.float32
        )
        grad_mid, grad_gain2 = rms_backward(mid_state, inverse2, norm2_gain, grad_normed2)
        grad_next = grad_next + grad_mid
        grad_attn = (grad_branch + grad_mid).astype(jnp.bfloat16)
        grad_out_w = jnp.einsum(
            "td,te->de", attended_low, grad_attn, preferred_element_type=jnp.float32
        )
        grad_attended = jnp.einsum(
            "te,de->td", grad_attn, w_out, preferred_element_type=jnp.float32
        ).astype(jnp.bfloat16)
        grad_query, grad_keys, grad_values = attention_backward(
            query_low, keys_all, values_all, allowed, log_total, grad_attended
        )
        local_keys, local_values = return_prior(grad_keys, grad_values, rows)
        grad_query_pre = (
            unrotate(grad_query.reshape(rows, -1, HD), cosine_tab, sine_tab)
            .reshape(rows, -1)
            .astype(jnp.bfloat16)
        )
        grad_key_pre = (
            unrotate(local_keys.reshape(rows, -1, HD), cosine_tab, sine_tab)
            .reshape(rows, -1)
            .astype(jnp.bfloat16)
        )
        grad_value_pre = local_values.astype(jnp.bfloat16)
        grad_query_w = jnp.einsum(
            "td,te->de", normed_low, grad_query_pre, preferred_element_type=jnp.float32
        )
        grad_key_w = jnp.einsum(
            "td,te->de", normed_low, grad_key_pre, preferred_element_type=jnp.float32
        )
        grad_value_w = jnp.einsum(
            "td,te->de", normed_low, grad_value_pre, preferred_element_type=jnp.float32
        )
        grad_normed = jnp.einsum(
            "te,de->td", grad_query_pre, w_query, preferred_element_type=jnp.float32
        )
        grad_normed = grad_normed + jnp.einsum(
            "te,de->td", grad_key_pre, w_key, preferred_element_type=jnp.float32
        )
        grad_normed = grad_normed + jnp.einsum(
            "te,de->td", grad_value_pre, w_value, preferred_element_type=jnp.float32
        )
        grad_input, grad_gain1 = rms_backward(state, inverse1, norm1_gain, grad_normed)
        grad_state = grad_next + grad_input
        level_pick = (jnp.arange(R) == level).astype(jnp.float32)
        grad_router = level_pick[:, None] * grad_router_row[None, :]
        level_grads = (
            grad_gain1,
            grad_query_w,
            grad_key_w,
            grad_value_w,
            grad_out_w,
            grad_gain2,
            grad_gate_w,
            grad_up_w,
            grad_down,
            grad_router,
        )
        shares = share_grads(level_grads)
        summed = shares if level == R - 1 else jax.tree.map(jnp.add, summed, shares)
    return (
        mixed,
        grad_state[None],
        summed[0],
        summed[1],
        summed[2],
        summed[3],
        summed[4],
        summed[5],
        summed[6],
        summed[7],
        summed[8],
        summed[9],
    )


def solution(mesh):
    in_specs = (
        P("str", "seq", None),
        P("str", None),
        P("str", "seq"),
        P("str", "seq", None),
        P(),
        P(),
        P(),
        P(),
        P(),
        P(),
        P(),
        P(),
        P(),
        P(),
    )
    out_specs = (
        P("str", "seq", None),
        P("str", "seq", None),
        P("str"),
        P("str", None),
        P("str", None),
        P("str", None),
        P("str", None),
        P("str"),
        P("str", None),
        P("str", None),
        P("str", None),
        P(None, "str"),
    )
    return jax.shard_map(
        per_device, mesh=mesh, in_specs=in_specs, out_specs=out_specs, check_vma=False
    )
```

profile of v0, /device:TPU:0, one launch (start us, length us, event | category | flops | bytes accessed | tf_op | source)
XLA Modules:
  0.0 2129.6 jit_solution(3205989772406738607)
XLA Ops:
  69.4 35.0 %while.84 = (s32[]{:T(128)}, bf16[5,256,3,64]{1,3,2,0:T(8,128)(2,1)}, f32[5,3,256]{2,1,0:T(4,128)S(1)}, bf16[5,1024,64]{1,2,0:T(8,128)(2,1)}, bf16[5,1024,64]{1,...) while((s32[]{:T(128)}, ...), condition=%wide.region_8.9_spmd.clone, body=%wide.region_5.8_spmd.clone.sunk | while | flops 212598016 | bytes 11084929 | solution.py:108
  144.9 33.0 %while.85 = (s32[]{:T(128)}, bf16[5,256,3,64]{1,3,2,0:T(8,128)(2,1)}, f32[5,3,256]{2,1,0:T(4,128)}, bf16[5,1024,64]{1,2,0:T(8,128)(2,1)}, bf16[5,1024,64]{1,2,0:...) while((s32[]{:T(128)}, ...), condition=%wide.region_14.15_spmd.clone, body=%wide.region_11.14_spmd.clone.sunk | while | flops 212598016 | bytes 11083389 | solution.py:108
  202.5 7.6 collective-permute-start.20
  223.5 33.3 %while.86 = (s32[]{:T(128)}, bf16[5,256,3,64]{1,3,2,0:T(8,128)(2,1)}, f32[5,3,256]{2,1,0:T(4,128)}, bf16[5,1024,64]{1,2,0:T(8,128)(2,1)}, bf16[5,1024,64]{1,2,0:...) while((s32[]{:T(128)}, ...), condition=%wide.region_20.21_spmd.clone, body=%wide.region_17.20_spmd.clone.sunk | while | flops 212598016 | bytes 11083389 | solution.py:108
  280.5 61.3 %while.87 = (s32[]{:T(128)}, f32[5,256,3,64]{1,3,2,0:T(8,128)}, f32[5,1024,64]{1,2,0:T(8,128)}, f32[5,1024,64]{1,2,0:T(8,128)}, bf16[5,1024,64]{1,2,0:T(8,128)(2...) while((s32[]{:T(128)}, f32[5,256,3,64]{1,3,2,0:T(8,128)}, ...), condition=%wide.region_26.27_spmd.clone, body=%wide.region_24.26_spmd.clone.sunk | while | flops 512343296 | bytes 25657496 | solution.py:119
  383.9 57.8 %while.88 = (s32[]{:T(128)}, f32[5,256,3,64]{1,3,2,0:T(8,128)S(1)}, f32[5,1024,64]{1,2,0:T(8,128)}, f32[5,1024,64]{1,2,0:T(8,128)}, bf16[5,1024,64]{1,2,0:T(8,12...) while((s32[]{:T(128)}, f32[5,256,3,64]{1,3,2,0:T(8,128)S(1)}, ...), condition=%wide.region_32.33_spmd.clone, body=%wide.region_30.32_spmd.clone.sunk | while | flops 512343296 | bytes 25657496 | solution.py:119
  469.4 10.2 collective-permute-done.38
  511.9 66.0 %while.89 = (s32[]{:T(128)}, f32[5,256,3,64]{1,3,2,0:T(8,128)}, f32[5,1024,64]{1,2,0:T(8,128)}, f32[5,1024,64]{1,2,0:T(8,128)}, bf16[5,1024,64]{1,2,0:T(8,128)(2...) while((s32[]{:T(128)}, f32[5,256,3,64]{1,3,2,0:T(8,128)}, ...), condition=%wide.region_38.39_spmd.clone, body=%wide.region_36.38_spmd.clone.sunk | while | flops 512343296 | bytes 25657496 | solution.py:119
  626.9 7.9 copy.102
  640.1 7.8 copy.104
  653.3 7.9 copy.106
  731.5 21.3 %reduce-scatter.85.cloned.1.call-done = bf16[640,960]{1,0:T(8,128)(2,1)} async-done(((bf16[2560,960]{1,0:T(8,128)(2,1)}), bf16[640,960]{1,0:T(8,128)(2,1)}) %reduce-scatter.85.cloned.1.call-update) | async-done | bytes 1228816
  755.2 94.2 %reduce-scatter.87.cloned.1.call-done = bf16[640,960]{1,0:T(8,128)(2,1)} async-done(((bf16[2560,960]{1,0:T(8,128)(2,1)}), bf16[640,960]{1,0:T(8,128)(2,1)}) %reduce-scatter.87.cloned.1.call-update) | async-done | bytes 1228816
  851.8 94.3 %reduce-scatter.89.cloned.1.call-done = bf16[640,960]{1,0:T(8,128)(2,1)} async-done(((bf16[2560,960]{1,0:T(8,128)(2,1)}), bf16[640,960]{1,0:T(8,128)(2,1)}) %reduce-scatter.89.cloned.1.call-update) | async-done | bytes 1228816
  948.5 41.9 %reduce-scatter.55.cloned.1.call-done = bf16[240,960]{1,0:T(8,128)(2,1)} async-done(((bf16[960,960]{1,0:T(8,128)(2,1)}), bf16[240,960]{1,0:T(8,128)(2,1)}) %reduce-scatter.55.cloned.1.call-update) | async-done | bytes 460816 | tf_op jit(solution)/shard_map/reduce_scatter | solution.py:172
  990.3 43.6 %reduce-scatter.49.cloned.1.call-done = bf16[240,960]{1,0:T(8,128)(2,1)} async-done(((bf16[960,960]{1,0:T(8,128)(2,1)}), bf16[240,960]{1,0:T(8,128)(2,1)}) %reduce-scatter.49.cloned.1.call-update) | async-done | bytes 460816 | tf_op jit(solution)/shard_map/reduce_scatter | solution.py:163
  1034.0 42.9 %reduce-scatter.57.cloned.1.call-done = bf16[240,960]{1,0:T(8,128)(2,1)} async-done(((bf16[960,960]{1,0:T(8,128)(2,1)}), bf16[240,960]{1,0:T(8,128)(2,1)}) %reduce-scatter.57.cloned.1.call-update) | async-done | bytes 460816 | tf_op jit(solution)/shard_map/reduce_scatter | solution.py:172
  1076.9 43.6 %reduce-scatter.51.cloned.1.call-done = bf16[240,960]{1,0:T(8,128)(2,1)} async-done(((bf16[960,960]{1,0:T(8,128)(2,1)}), bf16[240,960]{1,0:T(8,128)(2,1)}) %reduce-scatter.51.cloned.1.call-update) | async-done | bytes 460816 | tf_op jit(solution)/shard_map/reduce_scatter | solution.py:163
  1120.5 42.9 %reduce-scatter.59.cloned.1.call-done = bf16[240,960]{1,0:T(8,128)(2,1)} async-done(((bf16[960,960]{1,0:T(8,128)(2,1)}), bf16[240,960]{1,0:T(8,128)(2,1)}) %reduce-scatter.59.cloned.1.call-update) | async-done | bytes 460816 | tf_op jit(solution)/shard_map/reduce_scatter | solution.py:172
  1163.4 43.5 %reduce-scatter.53.cloned.1.call-done = bf16[240,960]{1,0:T(8,128)(2,1)} async-done(((bf16[960,960]{1,0:T(8,128)(2,1)}), bf16[240,960]{1,0:T(8,128)(2,1)}) %reduce-scatter.53.cloned.1.call-update) | async-done | bytes 460816 | tf_op jit(solution)/shard_map/reduce_scatter | solution.py:163
  1206.9 89.8 %reduce-scatter.61.cloned.1.call-done = bf16[240,2560]{1,0:T(8,128)(2,1)} async-done(((bf16[960,2560]{1,0:T(8,128)(2,1)}), bf16[240,2560]{1,0:T(8,128)(2,1)}) %reduce-scatter.61.cloned.1.call-update) | async-done | bytes 1228816 | tf_op jit(solution)/shard_map/reduce_scatter | solution.py:178
  1296.7 91.2 %reduce-scatter.67.cloned.1.call-done = bf16[240,2560]{1,0:T(8,128)(2,1)} async-done(((bf16[960,2560]{1,0:T(8,128)(2,1)}), bf16[240,2560]{1,0:T(8,128)(2,1)}) %reduce-scatter.67.cloned.1.call-update) | async-done | bytes 1228816 | tf_op jit(solution)/shard_map/reduce_scatter | solution.py:181
  1387.9 91.2 %reduce-scatter.63.cloned.1.call-done = bf16[240,2560]{1,0:T(8,128)(2,1)} async-done(((bf16[960,2560]{1,0:T(8,128)(2,1)}), bf16[240,2560]{1,0:T(8,128)(2,1)}) %reduce-scatter.63.cloned.1.call-update) | async-done | bytes 1228816 | tf_op jit(solution)/shard_map/reduce_scatter | solution.py:178
  1479.1 91.3 %reduce-scatter.69.cloned.1.call-done = bf16[240,2560]{1,0:T(8,128)(2,1)} async-done(((bf16[960,2560]{1,0:T(8,128)(2,1)}), bf16[240,2560]{1,0:T(8,128)(2,1)}) %reduce-scatter.69.cloned.1.call-update) | async-done | bytes 1228816 | tf_op jit(solution)/shard_map/reduce_scatter | solution.py:181
  1570.4 91.2 %reduce-scatter.65.cloned.1.call-done = bf16[240,2560]{1,0:T(8,128)(2,1)} async-done(((bf16[960,2560]{1,0:T(8,128)(2,1)}), bf16[240,2560]{1,0:T(8,128)(2,1)}) %reduce-scatter.65.cloned.1.call-update) | async-done | bytes 1228816 | tf_op jit(solution)/shard_map/reduce_scatter | solution.py:178
  1661.6 91.4 %reduce-scatter.71.cloned.1.call-done = bf16[240,2560]{1,0:T(8,128)(2,1)} async-done(((bf16[960,2560]{1,0:T(8,128)(2,1)}), bf16[240,2560]{1,0:T(8,128)(2,1)}) %reduce-scatter.71.cloned.1.call-update) | async-done | bytes 1228816 | tf_op jit(solution)/shard_map/reduce_scatter | solution.py:181
  1754.9 21.5 %reduce-scatter.91.cloned.1.call-done = bf16[240,3]{1,0:T(8,128)(2,1)} async-done(((bf16[960,3]{1,0:T(8,128)(2,1)}), bf16[240,3]{1,0:T(8,128)(2,1)}) %reduce-scatter.91.cloned.1.call-update) | async-done | bytes 1456
  1777.2 20.2 reduce-scatter.93.cloned.1.call-done
  1801.5 16.8 reduce-scatter.95.cloned.1.call-done
  1824.1 15.7 all-reduce.8
  1840.3 13.8 all-reduce.6
  1859.5 250.5 %all-reduce.11.cloned.1.call-done = (bf16[240,960]{1,0:T(8,128)(2,1)}, bf16[240,960]{1,0:T(8,128)(2,1)}, bf16[240,960]{1,0:T(8,128)(2,1)}, bf16[240,320]{0,1:T(8...) async-done(((bf16[240,960]{1,0:T(8,128)(2,1)}, ...) | async-done | bytes 14745616 | tf_op jit(solution)/shard_map/psum | solution.py:193
  (918 shorter events, 716.6 us)
Async XLA Ops:
  7.2 714.0 %reduce-scatter.79.cloned.1.call-start = ((), (), s32[]{:S(2)}) async-start(), calls=%async_computation.39 | async-start | bytes 921600
  8.7 34.1 %collective-permute-start.3 = (s32[256]{0:T(256)}, s32[256]{0:T(256)}, u32[]{:S(2)}, u32[]{:S(2)}) collective-permute-start(s32[256]{0:T(256)} %convert_element_type.671), channel_id=1, source_target_pairs={{0,12},{4,16},{8,20},{12,24},{16,28},{1,13},{5,17},{9,21},{13,25},... | collective-permute-start | bytes 3080 | tf_op jit(solution)/shard_map/ppermute | solution.py:19
  13.6 31.6 %collective-permute-start.4 = (s32[256]{0:T(256)}, s32[256]{0:T(256)}, u32[]{:S(2)}, u32[]{:S(2)}) collective-permute-start(s32[256]{0:T(256)} %convert_element_type.671), channel_id=1, source_target_pairs={{0,8},{4,12},{8,16},{12,20},{16,24},{20,28},{1,9},{5,13},{9,17},{1... | collective-permute-start | bytes 3080 | tf_op jit(solution)/shard_map/ppermute | solution.py:19
  17.5 29.0 %collective-permute-start.5 = (s32[256]{0:T(256)}, s32[256]{0:T(256)}, u32[]{:S(2)}, u32[]{:S(2)}) collective-permute-start(s32[256]{0:T(256)} %convert_element_type.671), channel_id=1, source_target_pairs={{0,4},{4,8},{8,12},{12,16},{16,20},{20,24},{24,28},{1,5},{5,9},{9,... | collective-permute-start | bytes 3080 | tf_op jit(solution)/shard_map/ppermute | solution.py:19
  19.8 29.8 %collective-permute-start.12 = (s32[256]{0:T(256)S(1)}, s32[256]{0:T(256)S(1)}, u32[]{:S(2)}, u32[]{:S(2)}) collective-permute-start(s32[256]{0:T(256)S(1)} %convert_element_type.685), channel_id=1, source_target_pairs={{0,12},{4,16},{8,20},{12,24},{16,28},{1,13},{5,17},{9,21},{13,25},... | collective-permute-start | bytes 3080 | tf_op jit(solution)/shard_map/ppermute | solution.py:19
  21.5 29.5 %collective-permute-start.13 = (s32[256]{0:T(256)S(1)}, s32[256]{0:T(256)}, u32[]{:S(2)}, u32[]{:S(2)}) collective-permute-start(s32[256]{0:T(256)S(1)} %convert_element_type.685), channel_id=1, source_target_pairs={{0,8},{4,12},{8,16},{12,20},{16,24},{20,28},{1,9},{5,13},{9,17},{1... | collective-permute-start | bytes 3080 | tf_op jit(solution)/shard_map/ppermute | solution.py:19
  443.9 25.5 %collective-permute-start.36 = (bf16[256,320]{0,1:T(8,128)(2,1)}, bf16[256,320]{0,1:T(8,128)(2,1)}, u32[]{:S(2)}, u32[]{:S(2)}) collective-permute-start(bf16[256,320]{0,1:T(8,128)(2,1)} %bitcast.87), channel_id=1, source_target_pairs={{4,0},{8,4},{12,8},{16,12},{20,16},{24,20},{28,24},{5,1},{9,5},{13... | collective-permute-start | bytes 491528 | tf_op jit(solution)/shard_map/ppermute | solution.py:19
  445.2 24.2 %collective-permute-start.37 = (bf16[256,320]{0,1:T(8,128)(2,1)}, bf16[256,320]{0,1:T(8,128)(2,1)}, u32[]{:S(2)}, u32[]{:S(2)}) collective-permute-start(bf16[256,320]{0,1:T(8,128)(2,1)} %bitcast.88), channel_id=1, source_target_pairs={{8,0},{12,4},{16,8},{20,12},{24,16},{28,20},{9,1},{13,5},{17,9},{2... | collective-permute-start | bytes 491528 | tf_op jit(solution)/shard_map/ppermute | solution.py:19
  448.8 274.2 %reduce-scatter.73.cloned.1.call-start = ((), (), s32[]{:S(2)}) async-start(), calls=%async_computation.36 | async-start | bytes 921600
  466.1 258.5 %reduce-scatter.81.cloned.1.call-start = ((), (), s32[]{:S(2)}) async-start(), calls=%async_computation.40 | async-start | bytes 921600
  508.4 218.0 %reduce-scatter.75.cloned.1.call-start = ((), (), s32[]{:S(2)}) async-start(), calls=%async_computation.37 | async-start | bytes 921600
  582.5 145.6 %reduce-scatter.83.cloned.1.call-start = ((), (), s32[]{:S(2)}) async-start(), calls=%async_computation.41 | async-start | bytes 921600
  602.4 127.4 %reduce-scatter.77.cloned.1.call-start = ((), (), s32[]{:S(2)}) async-start(), calls=%async_computation.38 | async-start | bytes 921600
  621.6 131.2 %reduce-scatter.85.cloned.1.call-start = ((), (), s32[]{:S(2)}) async-start(), calls=%async_computation.42 | async-start | bytes 6553600
  634.8 214.6 %reduce-scatter.87.cloned.1.call-start = ((), (), s32[]{:S(2)}) async-start(), calls=%async_computation.43 | async-start | bytes 6553600
  648.0 298.1 %reduce-scatter.89.cloned.1.call-start = ((), (), s32[]{:S(2)}) async-start(), calls=%async_computation.44 | async-start | bytes 6553600
  661.3 329.1 %reduce-scatter.55.cloned.1.call-start = ((), (), s32[]{:S(2)}) async-start(), calls=%async_computation.27 | async-start | bytes 2457600 | tf_op jit(solution)/shard_map/reduce_scatter | solution.py:172
  664.5 369.5 %reduce-scatter.49.cloned.1.call-start = ((), (), s32[]{:S(2)}) async-start(), calls=%async_computation.24 | async-start | bytes 2457600 | tf_op jit(solution)/shard_map/reduce_scatter | solution.py:163
  668.0 408.8 %reduce-scatter.57.cloned.1.call-start = ((), (), s32[]{:S(2)}) async-start(), calls=%async_computation.28 | async-start | bytes 2457600 | tf_op jit(solution)/shard_map/reduce_scatter | solution.py:172
  671.3 449.3 %reduce-scatter.51.cloned.1.call-start = ((), (), s32[]{:S(2)}) async-start(), calls=%async_computation.25 | async-start | bytes 2457600 | tf_op jit(solution)/shard_map/reduce_scatter | solution.py:163
  674.5 488.9 %reduce-scatter.59.cloned.1.call-start = ((), (), s32[]{:S(2)}) async-start(), calls=%async_computation.29 | async-start | bytes 2457600 | tf_op jit(solution)/shard_map/reduce_scatter | solution.py:172
  677.7 529.2 %reduce-scatter.53.cloned.1.call-start = ((), (), s32[]{:S(2)}) async-start(), calls=%async_computation.26 | async-start | bytes 2457600 | tf_op jit(solution)/shard_map/reduce_scatter | solution.py:163
  681.9 614.8 %reduce-scatter.61.cloned.1.call-start = ((), (), s32[]{:S(2)}) async-start(), calls=%async_computation.30 | async-start | bytes 6144000 | tf_op jit(solution)/shard_map/reduce_scatter | solution.py:178
  687.4 700.4 %reduce-scatter.67.cloned.1.call-start = ((), (), s32[]{:S(2)}) async-start(), calls=%async_computation.33 | async-start | bytes 6144000 | tf_op jit(solution)/shard_map/reduce_scatter | solution.py:181
  692.7 786.4 %reduce-scatter.63.cloned.1.call-start = ((), (), s32[]{:S(2)}) async-start(), calls=%async_computation.31 | async-start | bytes 6144000 | tf_op jit(solution)/shard_map/reduce_scatter | solution.py:178
  697.9 872.5 %reduce-scatter.69.cloned.1.call-start = ((), (), s32[]{:S(2)}) async-start(), calls=%async_computation.34 | async-start | bytes 6144000 | tf_op jit(solution)/shard_map/reduce_scatter | solution.py:181
  703.2 958.5 %reduce-scatter.65.cloned.1.call-start = ((), (), s32[]{:S(2)}) async-start(), calls=%async_computation.32 | async-start | bytes 6144000 | tf_op jit(solution)/shard_map/reduce_scatter | solution.py:178
  708.3 1044.6 %reduce-scatter.71.cloned.1.call-start = ((), (), s32[]{:S(2)}) async-start(), calls=%async_computation.35 | async-start | bytes 6144000 | tf_op jit(solution)/shard_map/reduce_scatter | solution.py:181
  713.7 1062.7 %reduce-scatter.91.cloned.1.call-start = ((), (), s32[]{:S(2)}) async-start(), calls=%async_computation.45 | async-start | bytes 307200
  717.3 1080.1 %reduce-scatter.93.cloned.1.call-start = ((), (), s32[]{:S(2)}) async-start(), calls=%async_computation.46 | async-start | bytes 307200
  719.3 1099.0 %reduce-scatter.95.cloned.1.call-start = ((), (), s32[]{:S(2)}) async-start(), calls=%async_computation.47 | async-start | bytes 307200
  720.9 1389.1 %all-reduce.11.cloned.1.call-start = ((), (), s32[]{:S(2)}) async-start(), calls=%async_computation.48 | async-start | bytes 29982720 | tf_op jit(solution)/shard_map/psum | solution.py:193
  (209 other events, 2054.7 us)
Sparse Core Ops, SparseCore 0:
  448.9 31.6 reduce-scatter.78
  482.9 22.1 reduce-scatter.72
  508.5 26.1 reduce-scatter.80
  582.6 26.1 reduce-scatter.74
  610.9 22.1 reduce-scatter.82
  635.3 22.1 reduce-scatter.76
  659.8 92.9 reduce-scatter.84
  755.1 94.2 reduce-scatter.86
  851.8 94.2 reduce-scatter.88
  948.2 42.0 reduce-scatter.54
  993.2 40.6 reduce-scatter.48
  1036.1 40.6 reduce-scatter.56
  1079.8 40.6 reduce-scatter.50
  1122.7 40.6 reduce-scatter.58
  1166.1 40.7 reduce-scatter.52
  1209.1 87.5 reduce-scatter.60
  1298.9 88.9 reduce-scatter.66
  1390.1 88.9 reduce-scatter.62
  1481.4 88.9 reduce-scatter.68
  1572.6 88.9 reduce-scatter.64
  1664.0 88.9 reduce-scatter.70
  1755.8 20.4 reduce-scatter.90
  1779.2 18.1 reduce-scatter.92
  1800.1 18.1 reduce-scatter.94
  1824.7 285.1 all-reduce.10
where the time goes:
time: 2140 us; the launch traced here: 2130 us
  waiting for transfers between devices  1370 us (64%)
  matrix products  386 us (18%)
  other arithmetic  115 us (5%)
  local copies, waits for them, and re-layouts  113 us (5%)
  starting transfers between devices  102 us (5%)
  blocking collectives  29.6 us (1%)
    reduce_scatter x3, waiting for transfers between devices, share_grads(): lax.psum_scatter(grads[7].astype(jnp.bfloat16), 'str', scatter_dimension=...  274 us
    reduce_scatter x3, waiting for transfers between devices, share_grads(): lax.psum_scatter(grads[6].astype(jnp.bfloat16), 'str', scatter_dimension=...  272 us
    unnamed x37, waiting for transfers between devices  269 us
    psum x1, waiting for transfers between devices, share_grads(): lax.psum(shares[1].astype(jnp.bfloat16), 'seq').astype(jnp.float32)  250 us
    reduce_scatter x3, waiting for transfers between devices, share_grads(): lax.psum_scatter(grads[1].astype(jnp.bfloat16), 'str', scatter_dimension=...  131 us
    reduce_scatter x3, waiting for transfers between devices, share_grads(): lax.psum_scatter(grads[4].astype(jnp.bfloat16), 'str', scatter_dimension=...  128 us
    ppermute x45, starting transfers between devices, shifted(): return lax.ppermute(block, axis, route)  100 us
    unnamed x376, local copies, waits for them, and re-layouts  80.3 us
  transfers between devices with their start and end apart: 70, of which 29 were waited for; matrix products, arithmetic and copies ran while one was open for 14% of the time, Pallas kernels for 0%

commit v1 on v0

v1 whole, which is shorter than its diff:
```python
import math

import jax
import jax.numpy as jnp
from jax import lax
from jax.sharding import PartitionSpec as P

HD = 64
R = 3
REACH = 3


EPSILON = 1e-05


def rms_forward(values, gain):
    inverse = lax.rsqrt(jnp.mean(values * values, axis=-1, keepdims=True) + EPSILON)
    return (values * inverse * gain, inverse)


def rms_backward(values, inverse, gain, grad_out):
    scaled = grad_out * gain
    grad_gain = jnp.sum(grad_out * values * inverse, axis=0)
    grad_in = inverse * scaled - values * inverse * inverse * inverse * jnp.mean(
        scaled * values, axis=-1, keepdims=True
    )
    return (grad_in, grad_gain)


def rotate(values, cosine_tab, sine_tab):
    half = values.shape[-1] // 2
    first = values[..., :half]
    second = values[..., half:]
    return jnp.concatenate(
        [first * cosine_tab - second * sine_tab, second * cosine_tab + first * sine_tab], -1
    )


def unrotate(grads, cosine_tab, sine_tab):
    half = grads.shape[-1] // 2
    first = grads[..., :half]
    second = grads[..., half:]
    return jnp.concatenate(
        [first * cosine_tab + second * sine_tab, second * cosine_tab - first * sine_tab], -1
    )


def doc_tables(positions, doc_lengths):
    ends = jnp.cumsum(doc_lengths, dtype=jnp.int32)
    after = positions[:, None] >= ends[None, :]
    doc_index = jnp.sum(after.astype(jnp.int32), axis=1, dtype=jnp.int32)
    offset = jnp.sum(jnp.where(after, doc_lengths[None, :], 0), axis=1, dtype=jnp.int32)
    return (doc_index, positions - offset)


def head_scores(query_grp, key_grp, allowed):
    scores = jnp.einsum(
        "qgd,td->gqt", query_grp, key_grp, preferred_element_type=jnp.float32
    ) * HD ** (-0.5)
    return jnp.where(allowed[None], scores, -1e30)


def attend_head(query_grp, key_grp, value_grp, allowed):
    scores = head_scores(query_grp, key_grp, allowed)
    peak = jnp.max(scores, axis=-1, keepdims=True)
    weights = jnp.exp(scores - peak)
    total = jnp.sum(weights, axis=-1, keepdims=True)
    probs = (weights / total).astype(jnp.bfloat16)
    output = jnp.einsum("gqt,td->qgd", probs, value_grp, preferred_element_type=jnp.float32)
    return (output, peak[..., 0] + jnp.log(total[..., 0]))


def attend_back(query_grp, key_grp, value_grp, allowed, log_total, grad_out):
    scores = head_scores(query_grp, key_grp, allowed)
    probs_full = jnp.exp(scores - log_total[..., None])
    probs = probs_full.astype(jnp.bfloat16)
    grad_probs = jnp.einsum("qgd,td->gqt", grad_out, value_grp, preferred_element_type=jnp.float32)
    grad_value = jnp.einsum("gqt,qgd->td", probs, grad_out, preferred_element_type=jnp.float32)
    delta = jnp.sum(probs_full * grad_probs, axis=-1, keepdims=True)
    grad_scores = (probs_full * (grad_probs - delta)).astype(jnp.bfloat16)
    grad_query = jnp.einsum(
        "gqt,td->qgd", grad_scores, key_grp, preferred_element_type=jnp.float32
    ) * HD ** (-0.5)
    grad_key = jnp.einsum(
        "gqt,qgd->td", grad_scores, query_grp, preferred_element_type=jnp.float32
    ) * HD ** (-0.5)
    return (grad_query, grad_key, grad_value)


def stack_heads(queries, keys_all, values_all):
    rows = queries.shape[0]
    kv_heads = keys_all.shape[1] // HD
    query_stack = queries.reshape(rows, kv_heads, -1, HD).transpose(1, 0, 2, 3)
    key_stack = keys_all.reshape(-1, kv_heads, HD).transpose(1, 0, 2)
    value_stack = values_all.reshape(-1, kv_heads, HD).transpose(1, 0, 2)
    return (query_stack, key_stack, value_stack)


def attention_forward(queries, keys_all, values_all, allowed):
    rows = queries.shape[0]
    stacks = stack_heads(queries, keys_all, values_all)
    outputs, log_total = lax.map(
        lambda group: attend_head(group[0], group[1], group[2], allowed), stacks
    )
    return (outputs.transpose(1, 0, 2, 3).reshape(rows, -1), log_total)


def attention_backward(queries, keys_all, values_all, allowed, log_total, grad_out):
    rows = queries.shape[0]
    kv_heads = keys_all.shape[1] // HD
    query_stack, key_stack, value_stack = stack_heads(queries, keys_all, values_all)
    grad_stack = grad_out.reshape(rows, kv_heads, -1, HD).transpose(1, 0, 2, 3)
    grad_query, grad_key, grad_value = lax.map(
        lambda group: attend_back(group[0], group[1], group[2], allowed, group[3], group[4]),
        (query_stack, key_stack, value_stack, log_total, grad_stack),
    )
    grad_query = grad_query.transpose(1, 0, 2, 3).reshape(rows, -1)
    grad_key = grad_key.transpose(1, 0, 2).reshape(-1, keys_all.shape[1])
    grad_value = grad_value.transpose(1, 0, 2).reshape(-1, keys_all.shape[1])
    return (grad_query, grad_key, grad_value)


def swap(block, mask):
    devices = range(lax.axis_size("seq"))
    return lax.ppermute(block, "seq", [(i, i ^ mask) for i in devices])


def moved(block, targets):
    devices = range(lax.axis_size("seq"))
    return lax.ppermute(
        block, "seq", [(i, t) for i, t in enumerate(targets) if t in devices]
    )


def halo(block):
    devices = range(lax.axis_size("seq"))
    even = lax.axis_index("seq") % 2 == 0
    two = moved(block, [i + 2 for i in devices])
    mixed = moved(block, [i + 1 if i % 2 == 0 else i + 3 for i in devices])
    across = swap(two, 1)
    return (jnp.where(even, mixed, across), two, jnp.where(even, across, mixed))


def halo_back(third, second, first):
    devices = range(lax.axis_size("seq"))
    even = lax.axis_index("seq") % 2 == 0
    across = swap(jnp.where(even, first, third).astype(jnp.bfloat16), 1)
    mixed = moved(
        jnp.where(even, third, first).astype(jnp.bfloat16),
        [i - 1 if i % 2 == 1 else i - 3 for i in devices],
    )
    both = (second + across.astype(jnp.float32)).astype(jnp.bfloat16)
    two = moved(both, [i - 2 for i in devices])
    return two.astype(jnp.float32) + mixed.astype(jnp.float32)


def bit_orders():
    devices = lax.axis_size("seq")
    rest = [1 << b for b in range(1, devices.bit_length() - 1)]
    half = len(rest) // 2
    return ([1] + rest, [1] + rest[half:] + rest[:half])


def relative(index, order):
    piece = jnp.zeros_like(index)
    for place, mask in enumerate(reversed(order)):
        piece = piece + ((index >> place) & 1) * mask
    return piece


def slot_rows(width):
    devices, streams = (lax.axis_size("seq"), lax.axis_size("str"))
    share = width // streams
    slots = -(-share // devices)
    return (share, -(-slots // 8) * 8)


def one_hot(rows, columns):
    return (rows[:, None] == columns[None, :]).astype(jnp.bfloat16)


def row_spread(width, order):
    devices, streams = (lax.axis_size("seq"), lax.axis_size("str"))
    share, slots = slot_rows(width)
    index = jnp.arange(devices * streams * slots, dtype=jnp.int32)
    slot = index % slots
    stream = (lax.axis_index("str") + (index // slots) % streams) % streams
    piece = relative(index // (slots * streams), order) ^ lax.axis_index("seq")
    inside = piece * slots + slot
    target = jnp.where(inside < share, stream * share + inside, -1)
    return one_hot(jnp.arange(width, dtype=jnp.int32), target)


def row_gather(width, order):
    devices = lax.axis_size("seq")
    share, slots = slot_rows(width)
    index = jnp.arange(devices * slots, dtype=jnp.int32)
    piece = relative(index // slots, order) ^ lax.axis_index("seq")
    return one_hot(jnp.arange(share, dtype=jnp.int32), piece * slots + index % slots)


def column_spread(width, order):
    devices = lax.axis_size("seq")
    used = -(-width // devices)
    lanes = -(-used // 128) * 128
    index = jnp.arange(devices * lanes, dtype=jnp.int32)
    piece = relative(index // lanes, order) ^ lax.axis_index("seq")
    slot = index % lanes
    target = jnp.where(slot < used, piece * used + slot, -1)
    return one_hot(jnp.arange(width, dtype=jnp.int32), target)


def low_dot(left, right):
    return jnp.dot(left, right, preferred_element_type=jnp.float32).astype(jnp.bfloat16)


def outer(left, right):
    return jnp.einsum("tm,tn->mn", left, right, preferred_element_type=jnp.float32)


def added(*terms):
    total = terms[0].astype(jnp.float32)
    for term in terms[1:]:
        total = total + term.astype(jnp.float32)
    return total.astype(jnp.bfloat16)


def reduce_rows(left, right, order):
    half = left.shape[1] // 2
    sent = outer(left[:, half:], right).astype(jnp.bfloat16)
    part = added(outer(left[:, :half], right), swap(sent, order[0]))
    for mask in order[1:]:
        half = part.shape[0] // 2
        part = added(part[:half], swap(part[half:], mask))
    streams = lax.axis_size("str")
    slots = part.shape[0] // streams
    terms = [part[:slots]]
    for distance in range(1, streams):
        route = [(i, (i + distance) % streams) for i in range(streams)]
        terms.append(
            lax.ppermute(part[distance * slots : (distance + 1) * slots], "str", route)
        )
    return added(*terms)


def collect_rows(part, order, width):
    for mask in reversed(order):
        part = jnp.concatenate([part, swap(part, mask)], 0)
    return jnp.dot(row_gather(width, order), part, preferred_element_type=jnp.float32)


def reduce_columns(left, right, order):
    half = right.shape[1] // 2
    sent = outer(left, right[:, half:]).astype(jnp.bfloat16)
    part = added(outer(left, right[:, :half]), swap(sent, order[0]))
    streams = lax.axis_size("str")
    here = lax.axis_index("str")
    route = [(i, (i + 1) % streams) for i in range(streams)]
    part = part.reshape(streams, -1, part.shape[1])

    def block(back):
        return lax.dynamic_index_in_dim(part, (here - back) % streams, 0, keepdims=False)

    running = block(1)
    for step in range(streams - 1):
        running = added(lax.ppermute(running, "str", route), block(step + 2))
    part = running
    for mask in order[1:]:
        half = part.shape[1] // 2
        part = added(part[:, :half], swap(part[:, half:], mask))
    return part


def collect_columns(part, order, width):
    for mask in reversed(order):
        part = jnp.concatenate([part, swap(part, mask)], 1)
    return jnp.einsum(
        "fm,dm->fd", part, column_spread(width, order), preferred_element_type=jnp.float32
    )


def stacked(values):
    return jnp.concatenate(values, 0)


def per_device(
    hidden,
    lengths,
    depth,
    cotangent,
    norm1_gain,
    w_query,
    w_key,
    w_value,
    w_out,
    norm2_gain,
    w_gate,
    w_up,
    w_down,
    router,
):
    rows, width = hidden.shape[1:]
    key_width = w_key.shape[1]
    seq_index = lax.axis_index("seq")
    local_pos = seq_index * rows + jnp.arange(rows, dtype=jnp.int32)
    key_pos = (seq_index - REACH) * rows + jnp.arange((REACH + 1) * rows, dtype=jnp.int32)
    doc_lengths = lengths[0]
    query_doc, place = doc_tables(local_pos, doc_lengths)
    key_doc, unused_place = doc_tables(key_pos, doc_lengths)
    base_mask = (
        (key_pos[None, :] >= 0)
        & (key_pos[None, :] <= local_pos[:, None])
        & (key_doc[None, :] == query_doc[:, None])
    )
    own_key = key_pos[None, :] == local_pos[:, None]
    half = HD // 2
    freqs = jnp.exp(-math.log(10000.0) * 2.0 * jnp.arange(half, dtype=jnp.float32) / HD)
    angles = place.astype(jnp.float32)[:, None, None] * freqs[None, None, :]
    cosine_tab = jnp.cos(angles)
    sine_tab = jnp.sin(angles)
    depth_row = depth[0]
    depth_all = jnp.concatenate([*halo(depth_row), depth_row], 0)
    router_rows = router.astype(jnp.float32)
    order_a, order_b = bit_orders()
    spread_a = row_spread(width, order_a)
    spread_b = row_spread(width, order_b)
    state = hidden[0].astype(jnp.float32)
    saved = []
    for level in range(R):
        normed, inverse1 = rms_forward(state, norm1_gain)
        normed_low = normed.astype(jnp.bfloat16)
        key_pre = jnp.dot(normed_low, w_key, preferred_element_type=jnp.float32)
        value_low = low_dot(normed_low, w_value)
        key_low = (
            rotate(key_pre.reshape(rows, -1, HD), cosine_tab, sine_tab)
            .reshape(rows, -1)
            .astype(jnp.bfloat16)
        )
        local_pair = jnp.concatenate([key_low, value_low], 1)
        pair = jnp.concatenate([*halo(local_pair), local_pair], 0)
        query_pre = jnp.dot(normed_low, w_query, preferred_element_type=jnp.float32)
        query_low = (
            rotate(query_pre.reshape(rows, -1, HD), cosine_tab, sine_tab)
            .reshape(rows, -1)
            .astype(jnp.bfloat16)
        )
        keys_all = pair[:, :key_width]
        values_all = pair[:, key_width:]
        allowed = base_mask & ((depth_all > level)[None, :] | own_key)
        attended, log_total = attention_forward(query_low, keys_all, values_all, allowed)
        attended_low = attended.astype(jnp.bfloat16)
        attn_out = jnp.dot(attended_low, w_out, preferred_element_type=jnp.float32)
        mid_state = state + attn_out
        normed2, inverse2 = rms_forward(mid_state, norm2_gain)
        normed2_low = normed2.astype(jnp.bfloat16)
        gate_pre = jnp.dot(normed2_low, w_gate, preferred_element_type=jnp.float32)
        up_pre = jnp.dot(normed2_low, w_up, preferred_element_type=jnp.float32)
        hidden_act = (jax.nn.silu(gate_pre) * up_pre).astype(jnp.bfloat16)
        ffn_out = jnp.dot(hidden_act, w_down, preferred_element_type=jnp.float32)
        gate_prob = jax.nn.sigmoid(
            jnp.dot(state, router_rows[level], precision=lax.Precision.HIGHEST)
        )
        active = (depth_row > level).astype(jnp.float32)
        both = attn_out + ffn_out
        saved.append(
            (
                state,
                inverse1,
                normed_low,
                query_low,
                keys_all,
                values_all,
                allowed,
                log_total,
                attended_low,
                mid_state,
                inverse2,
                normed2_low,
                gate_pre,
                up_pre,
                hidden_act,
                both,
                gate_prob,
                active,
            )
        )
        state = state + (active * gate_prob)[:, None] * both
    mixed = state.astype(jnp.bfloat16)[None]
    grad_state = cotangent[0]
    normed_spread = stacked([low_dot(item[2], spread_a) for item in saved])
    attended_spread = stacked([low_dot(item[8], spread_b) for item in saved])
    normed2_low = stacked([item[11] for item in saved])
    gate_spread = low_dot(normed2_low, spread_a)
    up_spread = low_dot(normed2_low, spread_b)
    hidden_cat = stacked([item[14] for item in saved])
    column_order = order_a
    spread_c = column_spread(width, column_order)
    factors = [[None] * R for kind in range(5)]
    down_part = None
    for level in range(R - 1, -1, -1):
        (
            state,
            inverse1,
            normed_low,
            query_low,
            keys_all,
            values_all,
            allowed,
            log_total,
            attended_low,
            mid_state,
            inverse2,
            unused_low,
            gate_pre,
            up_pre,
            hidden_act,
            both,
            gate_prob,
            active,
        ) = saved[level]
        grad_branch = (active * gate_prob)[:, None] * grad_state
        grad_logit = jnp.sum(grad_state * both, axis=-1) * active * gate_prob * (1.0 - gate_prob)
        grad_next = grad_state + grad_logit[:, None] * router_rows[level][None, :]
        grad_ffn = grad_branch.astype(jnp.bfloat16)
        factors[0][level] = low_dot(grad_ffn, spread_c)
        if level == 0:
            down_part = reduce_columns(hidden_cat, stacked(factors[0]), column_order)
        grad_act = jnp.einsum("td,fd->tf", grad_ffn, w_down, preferred_element_type=jnp.float32)
        sigma = jax.nn.sigmoid(gate_pre)
        grad_gate = (grad_act * up_pre * sigma * (1.0 + gate_pre * (1.0 - sigma))).astype(
            jnp.bfloat16
        )
        grad_up_pre = (grad_act * gate_pre * sigma).astype(jnp.bfloat16)
        factors[1][level] = grad_gate
        factors[2][level] = grad_up_pre
        if level == 0:
            gate_part = reduce_rows(gate_spread, stacked(factors[1]), order_a)
            up_part = reduce_rows(up_spread, stacked(factors[2]), order_b)
        grad_normed2 = jnp.einsum(
            "tf,df->td", grad_gate, w_gate, preferred_element_type=jnp.float32
        )
        grad_normed2 = grad_normed2 + jnp.einsum(
            "tf,df->td", grad_up_pre, w_up, preferred_element_type=jnp.float32
        )
        grad_mid, unused_gain = rms_backward(mid_state, inverse2, norm2_gain, grad_normed2)
        grad_next = grad_next + grad_mid
        grad_attn = (grad_branch + grad_mid).astype(jnp.bfloat16)
        factors[3][level] = grad_attn
        if level == 0:
            out_part = reduce_rows(attended_spread, stacked(factors[3]), order_b)
        grad_attended = jnp.einsum(
            "te,de->td", grad_attn, w_out, preferred_element_type=jnp.float32
        ).astype(jnp.bfloat16)
        grad_query, grad_keys, grad_values = attention_backward(
            query_low, keys_all, values_all, allowed, log_total, grad_attended
        )
        grad_pair = jnp.concatenate([grad_keys, grad_values], 1)
        local_pair = grad_pair[REACH * rows :] + halo_back(
            grad_pair[:rows], grad_pair[rows : 2 * rows], grad_pair[2 * rows : 3 * rows]
        )
        grad_query_pre = (
            unrotate(grad_query.reshape(rows, -1, HD), cosine_tab, sine_tab)
            .reshape(rows, -1)
            .astype(jnp.bfloat16)
        )
        grad_key_pre = (
            unrotate(local_pair[:, :key_width].reshape(rows, -1, HD), cosine_tab, sine_tab)
            .reshape(rows, -1)
            .astype(jnp.bfloat16)
        )
        grad_value_pre = local_pair[:, key_width:].astype(jnp.bfloat16)
        router_term = (grad_logit / inverse1[:, 0])[:, None] * (
            jnp.arange(R)[None, :] == level
        ).astype(jnp.float32)
        factors[4][level] = jnp.concatenate(
            [grad_query_pre, grad_key_pre, grad_value_pre, router_term.astype(jnp.bfloat16)], 1
        )
        grad_normed = jnp.einsum(
            "te,de->td", grad_query_pre, w_query, preferred_element_type=jnp.float32
        )
        grad_normed = grad_normed + jnp.einsum(
            "te,de->td", grad_key_pre, w_key, preferred_element_type=jnp.float32
        )
        grad_normed = grad_normed + jnp.einsum(
            "te,de->td", grad_value_pre, w_value, preferred_element_type=jnp.float32
        )
        grad_input, unused_gain = rms_backward(state, inverse1, norm1_gain, grad_normed)
        grad_state = grad_next + grad_input
    front_part = reduce_rows(normed_spread, stacked(factors[4]), order_a)
    down_sum = collect_columns(down_part, column_order, width)
    gate_sum = collect_rows(gate_part, order_a, width)
    up_sum = collect_rows(up_part, order_b, width)
    out_sum = collect_rows(out_part, order_b, width)
    front_sum = collect_rows(front_part, order_a, width)
    share = gate_sum.shape[0]
    first = lax.axis_index("str") * share

    def mine(table):
        return lax.dynamic_slice_in_dim(table, first, share, 0)

    gain1, gain2 = (mine(norm1_gain), mine(norm2_gain))
    query_sum = front_sum[:, :width]
    key_sum = front_sum[:, width : width + key_width]
    value_sum = front_sum[:, width + key_width : width + 2 * key_width]
    router_sum = (front_sum[:, width + 2 * key_width :] / gain1[:, None]).T

    def row_dots(weights, sums):
        return jnp.sum(mine(weights).astype(jnp.float32) * sums, axis=1)

    gain1_sum = (
        row_dots(w_query, query_sum) + row_dots(w_key, key_sum) + row_dots(w_value, value_sum)
    ) / gain1
    gain2_sum = (row_dots(w_gate, gate_sum) + row_dots(w_up, up_sum)) / gain2
    return (
        mixed,
        grad_state[None],
        gain1_sum,
        query_sum,
        key_sum,
        value_sum,
        out_sum,
        gain2_sum,
        gate_sum,
        up_sum,
        down_sum,
        router_sum,
    )


def solution(mesh):
    in_specs = (
        P("str", "seq", None),
        P("str", None),
        P("str", "seq"),
        P("str", "seq", None),
        P(),
        P(),
        P(),
        P(),
        P(),
        P(),
        P(),
        P(),
        P(),
        P(),
    )
    out_specs = (
        P("str", "seq", None),
        P("str", "seq", None),
        P("str"),
        P("str", None),
        P("str", None),
        P("str", None),
        P("str", None),
        P("str"),
        P("str", None),
        P("str", None),
        P("str", None),
        P(None, "str"),
    )
    return jax.shard_map(
        per_device, mesh=mesh, in_specs=in_specs, out_specs=out_specs, check_vma=False
    )
```

time: 2140 us -> 822 us (0.38)
  waiting for transfers between devices: 1370 us -> 124 us
  starting transfers between devices: 102 us -> 178 us
  matrix products: 386 us -> 321 us
  local copies, waits for them, and re-layouts: 113 us -> 51.7 us
  blocking collectives: 29.6 us -> 0 us
    reduce_scatter x12 -> x0, waiting for transfers between devices: 804 us -> none  [the longest x3 274 us: share_grads(): lax.psum_scatter(grads[7].astype(jnp.bfloat16), 'str', scatter_dimension=...]
    unnamed x37 -> x0, waiting for transfers between devices: 269 us -> none
    psum x1 -> x0, waiting for transfers between devices: 250 us -> none  [share_grads(): lax.psum(shares[1].astype(jnp.bfloat16), 'seq').astype(jnp.float32)]
    ppermute x45 -> x66, waiting for transfers between devices: 41.6 us -> 124 us  [the longest x37 52.5 us: swap(): return lax.ppermute(block, 'seq', [(i, i ^ mask) for i in devices])]
    ppermute x45 -> x66, starting transfers between devices: 100 us -> 178 us  [the longest x12 61.7 us: reduce_rows(): lax.ppermute(part[distance * slots:(distance + 1) * slots], 'str', route)]
    unnamed x376 -> x444, local copies, waits for them, and re-layouts: 80.3 us -> 19.5 us
    dot_general x48 -> x50, matrix products: 128 us -> 103 us  [the longest x14 22.8 us: low_dot(): jnp.dot(left, right, preferred_element_type=jnp.float32)]
    concatenate x6 -> x20, other arithmetic: 4.76 us -> 27.9 us  [the longest x4 20.8 us: stacked(): return jnp.concatenate(values, 0)]
  transfers between devices with their start and end apart: 70 -> 66, of which waited for: 29 -> 24; matrix products, arithmetic and copies ran while one was open for 14% -> 14% of each run, Pallas kernels for 0% -> 0%
where the time goes in v1:
time: 822 us; the launch traced here: 811 us
  matrix products  321 us (39%)
  starting transfers between devices  178 us (22%)
  other arithmetic  130 us (16%)
  waiting for transfers between devices  124 us (15%)
  local copies, waits for them, and re-layouts  51.7 us (6%)
    ppermute x12, starting transfers between devices, reduce_rows(): lax.ppermute(part[distance * slots:(distance + 1) * slots], 'str', route)  61.7 us
    dot_general x30, matrix products, head_scores(): jnp.einsum('qgd,td->gqt', query_grp, key_grp, preferred_element_type=jnp....  55.7 us
    ppermute x3, starting transfers between devices, reduce_columns(): running = added(lax.ppermute(running, 'str', route), block(step + 2))  52.6 us
    ppermute x37, waiting for transfers between devices, swap(): return lax.ppermute(block, 'seq', [(i, i ^ mask) for i in devices])  52.5 us
    ppermute x14, waiting for transfers between devices, moved(): lax.ppermute(block, 'seq', [(i, t) for i, t in enumerate(targets) if t in...  33.7 us
    ppermute x14, starting transfers between devices, moved(): lax.ppermute(block, 'seq', [(i, t) for i, t in enumerate(targets) if t in...  33.2 us
    and x30, other arithmetic, per_device(): allowed = base_mask & ((depth_all > level)[None, :] | own_key)  32.3 us
    ppermute x37, starting transfers between devices, swap(): return lax.ppermute(block, 'seq', [(i, i ^ mask) for i in devices])  30.7 us
  transfers between devices with their start and end apart: 66, of which 24 were waited for; matrix products, arithmetic and copies ran while one was open for 14% of the time, Pallas kernels for 0%

profile of v1, /device:TPU:0, one launch (start us, length us, event | category | flops | bytes accessed | tf_op | source)
XLA Modules:
  0.0 810.6 jit_solution(4419335739263122633)
XLA Ops:
  8.2 5.6 collective-permute-start.1
  46.1 30.2 %while.84 = (s32[]{:T(128)}, bf16[5,256,3,64]{1,3,2,0:T(8,128)(2,1)S(1)}, f32[5,3,256]{2,1,0:T(4,128)}, bf16[5,1024,64]{1,2,0:T(8,128)(2,1)}, bf16[5,1024,64]{1,...) while((s32[]{:T(128)}, ...), condition=%wide.region_8.9_spmd.clone, body=%wide.region_5.8_spmd.clone.sunk | while | flops 212598016 | bytes 11085437 | solution.py:102
  82.4 6.7 multiply_convert_fusion.8
  108.5 30.7 %while.85 = (s32[]{:T(128)}, bf16[5,256,3,64]{1,3,2,0:T(8,128)(2,1)S(1)}, f32[5,3,256]{2,1,0:T(4,128)}, bf16[5,1024,64]{1,2,0:T(8,128)(2,1)}, bf16[5,1024,64]{1,...) while((s32[]{:T(128)}, ...), condition=%wide.region_14.15_spmd.clone, body=%wide.region_11.14_spmd.clone.sunk | while | flops 212598016 | bytes 11085437 | solution.py:102
  145.6 6.7 multiply_convert_fusion.7
  157.0 4.5 collective-permute-start.10
  173.7 30.5 %while.86 = (s32[]{:T(128)}, bf16[5,256,3,64]{1,3,2,0:T(8,128)(2,1)S(1)}, f32[5,3,256]{2,1,0:T(4,128)}, bf16[5,1024,64]{1,2,0:T(8,128)(2,1)}, bf16[5,1024,64]{1,...) while((s32[]{:T(128)}, ...), condition=%wide.region_20.21_spmd.clone, body=%wide.region_17.20_spmd.clone.sunk | while | flops 212598016 | bytes 11085437 | solution.py:102
  232.8 56.3 %while.87 = (s32[]{:T(128)}, f32[5,256,3,64]{1,3,2,0:T(8,128)}, f32[5,1024,64]{1,2,0:T(8,128)}, f32[5,1024,64]{1,2,0:T(8,128)}, bf16[5,1024,64]{1,2,0:T(8,128)(2...) while((s32[]{:T(128)}, f32[5,256,3,64]{1,3,2,0:T(8,128)}, ...), condition=%wide.region_26.27_spmd.clone, body=%wide.region_24.26_spmd.clone.sunk | while | flops 512343296 | bytes 25657496 | solution.py:113
  302.7 9.8 %collective-permute-done.13 = bf16[256,640]{0,1:T(8,128)(2,1)S(1)} collective-permute-done((bf16[256,640]{0,1:T(8,128)(2,1)S(1)}, bf16[256,640]{0,1:T(8,128)(2,1)S(1)}, u32[]{:S(2)}, u32[]{:S(2)}) %collective-permute-start.13) | collective-permute-done | bytes 327712 | tf_op jit(solution)/shard_map/ppermute | solution.py:130
  329.6 57.7 %while.88 = (s32[]{:T(128)}, f32[5,256,3,64]{1,3,2,0:T(8,128)}, f32[5,1024,64]{1,2,0:T(8,128)S(1)}, f32[5,1024,64]{1,2,0:T(8,128)}, bf16[5,1024,64]{1,2,0:T(8,12...) while((s32[]{:T(128)}, f32[5,256,3,64]{1,3,2,0:T(8,128)}, ...), condition=%wide.region_32.33_spmd.clone, body=%wide.region_30.32_spmd.clone.sunk | while | flops 512343296 | bytes 25657496 | solution.py:113
  399.1 8.4 %collective-permute-done.16 = bf16[256,640]{0,1:T(8,128)(2,1)S(1)} collective-permute-done((bf16[256,640]{0,1:T(8,128)(2,1)S(1)}, bf16[256,640]{0,1:T(8,128)(2,1)S(1)}, u32[]{:S(2)}, u32[]{:S(2)}) %collective-permute-start.16) | collective-permute-done | bytes 327712 | tf_op jit(solution)/shard_map/ppermute | solution.py:130
  425.8 57.6 %while.89 = (s32[]{:T(128)}, f32[5,256,3,64]{1,3,2,0:T(8,128)}, f32[5,1024,64]{1,2,0:T(8,128)S(1)}, f32[5,1024,64]{1,2,0:T(8,128)}, bf16[5,1024,64]{1,2,0:T(8,12...) while((s32[]{:T(128)}, f32[5,256,3,64]{1,3,2,0:T(8,128)}, ...), condition=%wide.region_38.39_spmd.clone, body=%wide.region_36.38_spmd.clone.sunk | while | flops 512343296 | bytes 25657496 | solution.py:113
  502.9 10.2 %collective-permute-done.19 = bf16[256,640]{0,1:T(8,128)(2,1)S(1)} collective-permute-done((bf16[256,640]{0,1:T(8,128)(2,1)S(1)}, bf16[256,640]{0,1:T(8,128)(2,1)S(1)}, u32[]{:S(2)}, u32[]{:S(2)}) %collective-permute-start.19) | collective-permute-done | bytes 327712 | tf_op jit(solution)/shard_map/ppermute | solution.py:130
  516.8 18.1 %maximum_maximum_fusion = bf16[768,1603]{0,1:T(8,128)(2,1)S(1)} fusion(bf16[256,3]{0,1:T(4,128)(2,1)S(1)} %copy-done.141, bf16[256,320]{0,1:T(8,128)(2,1)S(1)} %copy-done.83, bf16[256,320]{0,1:T(8,128)(2,1)S(1)} %bitcast.787, bf16[256,960]{0,1:T(8,128)(2,1)S(1)} %bitcast.775, bf16[256,3]{0,1:T(4,128)(2,1)S(1)} %copy-done.142, ...), kind=kLoop, calls=%fused_computation.250 | loop fusion | flops 29546496 | bytes 4924416 | tf_op jit(solution)/shard_map/concatenate | solution.py:283
  548.9 4.5 collective-permute-done.33
  553.4 8.1 collective-permute-done.34
  564.3 6.1 collective-permute-done.36
  572.2 6.1 collective-permute-done.37
  587.5 4.8 collective-permute-start.58
  592.3 11.8 %collective-permute-done.22 = bf16[256,1603]{0,1:T(8,128)(2,1)S(1)} collective-permute-done((bf16[256,1603]{0,1:T(8,128)(2,1)S(1)}, bf16[256,1603]{0,1:T(8,128)(2,1)S(1)}, u32[]{:S(2)}, u32[]{:S(2)}) %collective-permute-start.22) | collective-permute-done | bytes 820768 | tf_op jit(solution)/shard_map/ppermute | solution.py:125
  610.5 6.3 collective-permute-done.23
  617.4 4.8 collective-permute-start.24
  625.0 9.7 %collective-permute-done.24 = bf16[32,1603]{0,1:T(8,128)(2,1)S(1)} collective-permute-done((bf16[32,1603]{0,1:T(8,128)(2,1)S(1)}, bf16[32,1603]{0,1:T(8,128)(2,1)S(1)}, u32[]{:S(2)}, u32[]{:S(2)}) %collective-permute-start.24) | collective-permute-done | bytes 102624 | tf_op jit(solution)/shard_map/ppermute | solution.py:241
  634.7 13.1 %collective-permute-start.59 = (bf16[640,512]{1,0:T(8,128)(2,1)S(1)}, bf16[640,512]{1,0:T(8,128)(2,1)S(1)}, u32[]{:S(2)}, u32[]{:S(2)}) collective-permute-start(bf16[640,512]{1,0:T(8,128)(2,1)S(1)} %fusion.231), channel_id=1, source_target_pairs={{0,1},{1,2},{2,3},{3,0},{4,5},{5,6},{6,7},{7,4},{8,9},{9,10},{10,1... | collective-permute-start | bytes 1966088 | tf_op jit(solution)/shard_map/ppermute | solution.py:266
  647.8 4.5 collective-permute-done.25
  658.2 5.6 collective-permute-done.27
  665.8 34.6 %collective-permute-start.60 = (bf16[640,512]{1,0:T(8,128)(2,1)S(1)}, bf16[640,512]{1,0:T(8,128)(2,1)S(1)}, u32[]{:S(2)}, u32[]{:S(2)}) collective-permute-start(bf16[640,512]{1,0:T(8,128)(2,1)S(1)} %fusion.230), channel_id=1, source_target_pairs={{0,1},{1,2},{2,3},{3,0},{4,5},{5,6},{6,7},{7,4},{8,9},{9,10},{10,1... | collective-permute-start | bytes 1966088 | tf_op jit(solution)/shard_map/ppermute | solution.py:266
  706.0 7.4 collective-permute-done.60
  718.1 27.6 %collective-permute-start.51 = (bf16[32,2560]{1,0:T(8,128)(2,1)S(1)}, bf16[32,2560]{1,0:T(8,128)(2,1)S(1)}, u32[]{:S(2)}, u32[]{:S(2)}) collective-permute-start(bf16[32,2560]{1,0:T(8,128)(2,1)S(1)} %get-tuple-element.788), channel_id=1, source_target_pairs={{0,1},{1,2},{2,3},{3,0},{4,5},{5,6},{6,7},{7,4},{8,9},{9,10},{10,1... | collective-permute-start | bytes 491528 | tf_op jit(solution)/shard_map/ppermute | solution.py:241
  750.3 10.5 %collective-permute-start.43 = (bf16[32,2560]{1,0:T(8,128)(2,1)S(1)}, bf16[32,2560]{1,0:T(8,128)(2,1)S(1)}, u32[]{:S(2)}, u32[]{:S(2)}) collective-permute-start(bf16[32,2560]{1,0:T(8,128)(2,1)S(1)} %get-tuple-element.793), channel_id=1, source_target_pairs={{0,2},{1,3},{2,0},{3,1},{4,6},{5,7},{6,4},{7,5},{8,10},{9,11},{10,... | collective-permute-start | bytes 491528 | tf_op jit(solution)/shard_map/ppermute | solution.py:241
  762.2 6.6 collective-permute-start.44
  775.1 5.3 collective-permute-done.62
  (997 shorter events, 556.9 us)
Async XLA Ops:
  8.2 31.8 %collective-permute-start.1 = (bf16[256,640]{0,1:T(8,128)(2,1)}, bf16[256,640]{0,1:T(8,128)(2,1)}, u32[]{:S(2)}, u32[]{:S(2)}) collective-permute-start(bf16[256,640]{0,1:T(8,128)(2,1)} %pad_maximum_fusion.38), channel_id=1, source_target_pairs={{0,8},{4,12},{8,16},{12,20},{16,24},{20,28},{1,9},{5,13},{9,17},{1... | collective-permute-start | bytes 983048 | tf_op jit(solution)/shard_map/ppermute | solution.py:130
  13.8 28.1 %collective-permute-start = (bf16[256,640]{0,1:T(8,128)(2,1)}, bf16[256,640]{0,1:T(8,128)(2,1)}, u32[]{:S(2)}, u32[]{:S(2)}) collective-permute-start(bf16[256,640]{0,1:T(8,128)(2,1)} %pad_maximum_fusion.38), channel_id=1, source_target_pairs={{0,4},{4,16},{8,12},{12,24},{16,20},{24,28},{1,5},{5,17},{9,13},{1... | collective-permute-start | bytes 983048 | tf_op jit(solution)/shard_map/ppermute | solution.py:130
  16.0 22.4 %collective-permute-start.4 = (s32[256]{0:T(256)S(1)}, s32[256]{0:T(256)}, u32[]{:S(2)}, u32[]{:S(2)}) collective-permute-start(s32[256]{0:T(256)S(1)} %bitcast.797), channel_id=1, source_target_pairs={{0,8},{4,12},{8,16},{12,20},{16,24},{20,28},{1,9},{5,13},{9,17},{1... | collective-permute-start | bytes 3080 | tf_op jit(solution)/shard_map/ppermute | solution.py:130
  19.2 21.3 %collective-permute-start.3 = (s32[256]{0:T(256)S(1)}, s32[256]{0:T(256)}, u32[]{:S(2)}, u32[]{:S(2)}) collective-permute-start(s32[256]{0:T(256)S(1)} %bitcast.798), channel_id=1, source_target_pairs={{0,4},{4,16},{8,12},{12,24},{16,20},{24,28},{1,5},{5,17},{9,13},{1... | collective-permute-start | bytes 3080 | tf_op jit(solution)/shard_map/ppermute | solution.py:130
  486.3 16.6 %collective-permute-start.20 = (bf16[256,640]{0,1:T(8,128)(2,1)S(1)}, bf16[256,640]{0,1:T(8,128)(2,1)S(1)}, u32[]{:S(2)}, u32[]{:S(2)}) collective-permute-start(bf16[256,640]{0,1:T(8,128)(2,1)S(1)} %select_convert_fusion), channel_id=1, source_target_pairs={{4,0},{12,8},{16,4},{20,16},{24,12},{28,24},{5,1},{13,9},{17,5},{2... | collective-permute-start | bytes 983048 | tf_op jit(solution)/shard_map/ppermute | solution.py:130
  490.9 94.0 %collective-permute-start.57 = (bf16[2560,512]{1,0:T(8,128)(2,1)S(1)}, bf16[2560,512]{1,0:T(8,128)(2,1)S(1)}, u32[]{:S(2)}, u32[]{:S(2)}) collective-permute-start(bf16[2560,512]{1,0:T(8,128)(2,1)S(1)} %convolution_convert_fusion), channel_id=1, source_target_pairs={{0,4},{4,0},{8,12},{12,8},{16,20},{20,16},{24,28},{28,24},{1,5},{5... | collective-permute-start | bytes 7864328 | tf_op jit(solution)/shard_map/ppermute | solution.py:125
  498.2 16.2 %collective-permute-start.30 = (bf16[512,960]{0,1:T(8,128)(2,1)S(1)}, bf16[512,960]{0,1:T(8,128)(2,1)S(1)}, u32[]{:S(2)}, u32[]{:S(2)}) collective-permute-start(bf16[512,960]{0,1:T(8,128)(2,1)S(1)} %convolution_convert_fusion.4), channel_id=1, source_target_pairs={{0,4},{4,0},{8,12},{12,8},{16,20},{20,16},{24,28},{28,24},{1,5},{5... | collective-permute-start | bytes 2949128 | tf_op jit(solution)/shard_map/ppermute | solution.py:125
  515.4 19.5 %collective-permute-start.31 = (bf16[256,960]{0,1:T(8,128)(2,1)S(1)}, bf16[256,960]{0,1:T(8,128)(2,1)S(1)}, u32[]{:S(2)}, u32[]{:S(2)}) collective-permute-start(bf16[256,960]{0,1:T(8,128)(2,1)S(1)} %slice.492), channel_id=1, source_target_pairs={{0,16},{4,20},{8,24},{12,28},{16,0},{20,4},{24,8},{28,12},{1,17},{... | collective-permute-start | bytes 1474568 | tf_op jit(solution)/shard_map/ppermute | solution.py:125
  538.1 43.7 %collective-permute-start.21 = (bf16[512,1603]{0,1:T(8,128)(2,1)S(1)}, bf16[512,1603]{0,1:T(8,128)(2,1)S(1)}, u32[]{:S(2)}, u32[]{:S(2)}) collective-permute-start(bf16[512,1603]{0,1:T(8,128)(2,1)S(1)} %convolution_convert_fusion.3), channel_id=1, source_target_pairs={{0,4},{4,0},{8,12},{12,8},{16,20},{20,16},{24,28},{28,24},{1,5},{5... | collective-permute-start | bytes 4924424 | tf_op jit(solution)/shard_map/ppermute | solution.py:125
  544.3 17.2 %collective-permute-start.34 = (bf16[32,960]{0,1:T(8,128)(2,1)S(1)}, bf16[32,960]{0,1:T(8,128)(2,1)S(1)}, u32[]{:S(2)}, u32[]{:S(2)}) collective-permute-start(bf16[32,960]{0,1:T(8,128)(2,1)S(1)} %get-tuple-element.817), channel_id=1, source_target_pairs={{0,2},{1,3},{2,0},{3,1},{4,6},{5,7},{6,4},{7,5},{8,10},{9,11},{10,... | collective-permute-start | bytes 184328 | tf_op jit(solution)/shard_map/ppermute | solution.py:241
  546.9 14.6 %collective-permute-start.35 = (bf16[32,960]{0,1:T(8,128)(2,1)S(1)}, bf16[32,960]{0,1:T(8,128)(2,1)S(1)}, u32[]{:S(2)}, u32[]{:S(2)}) collective-permute-start(bf16[32,960]{0,1:T(8,128)(2,1)S(1)} %get-tuple-element.816), channel_id=1, source_target_pairs={{0,3},{1,0},{2,1},{3,2},{4,7},{5,4},{6,5},{7,6},{8,11},{9,8},{10,9... | collective-permute-start | bytes 184328 | tf_op jit(solution)/shard_map/ppermute | solution.py:241
  553.4 52.5 %collective-permute-start.48 = (bf16[512,2560]{1,0:T(8,128)(2,1)S(1)}, bf16[512,2560]{1,0:T(8,128)(2,1)}, u32[]{:S(2)}, u32[]{:S(2)}) collective-permute-start(bf16[512,2560]{1,0:T(8,128)(2,1)S(1)} %convolution_convert_fusion.1), channel_id=1, source_target_pairs={{0,4},{4,0},{8,12},{12,8},{16,20},{20,16},{24,28},{28,24},{1,5},{5... | collective-permute-start | bytes 7864328 | tf_op jit(solution)/shard_map/ppermute | solution.py:125
  561.5 92.6 %collective-permute-start.39 = (bf16[512,2560]{1,0:T(8,128)(2,1)S(1)}, bf16[512,2560]{1,0:T(8,128)(2,1)S(1)}, u32[]{:S(2)}, u32[]{:S(2)}) collective-permute-start(bf16[512,2560]{1,0:T(8,128)(2,1)S(1)} %convolution_convert_fusion.2), channel_id=1, source_target_pairs={{0,4},{4,0},{8,12},{12,8},{16,20},{20,16},{24,28},{28,24},{1,5},{5... | collective-permute-start | bytes 7864328 | tf_op jit(solution)/shard_map/ppermute | solution.py:125
  583.4 20.8 %collective-permute-start.22 = (bf16[256,1603]{0,1:T(8,128)(2,1)S(1)}, bf16[256,1603]{0,1:T(8,128)(2,1)S(1)}, u32[]{:S(2)}, u32[]{:S(2)}) collective-permute-start(bf16[256,1603]{0,1:T(8,128)(2,1)S(1)} %slice.479), channel_id=1, source_target_pairs={{0,8},{4,12},{8,0},{12,4},{16,24},{20,28},{24,16},{28,20},{1,9},{5... | collective-permute-start | bytes 2462216 | tf_op jit(solution)/shard_map/ppermute | solution.py:125
  587.5 37.3 %collective-permute-start.58 = (bf16[640,512]{1,0:T(8,128)(2,1)S(1)}, bf16[640,512]{1,0:T(8,128)(2,1)S(1)}, u32[]{:S(2)}, u32[]{:S(2)}) collective-permute-start(bf16[640,512]{1,0:T(8,128)(2,1)S(1)} %dynamic-slice_bitcast_fusion.3), channel_id=1, source_target_pairs={{0,1},{1,2},{2,3},{3,0},{4,5},{5,6},{6,7},{7,4},{8,9},{9,10},{10,1... | collective-permute-start | bytes 1966088 | tf_op jit(solution)/shard_map/ppermute | solution.py:266
  609.8 90.6 %collective-permute-start.49 = (bf16[256,2560]{1,0:T(8,128)(2,1)S(1)}, bf16[256,2560]{1,0:T(8,128)(2,1)S(1)}, u32[]{:S(2)}, u32[]{:S(2)}) collective-permute-start(bf16[256,2560]{1,0:T(8,128)(2,1)S(1)} %slice.512), channel_id=1, source_target_pairs={{0,16},{4,20},{8,24},{12,28},{16,0},{20,4},{24,8},{28,12},{1,17},{... | collective-permute-start | bytes 3932168 | tf_op jit(solution)/shard_map/ppermute | solution.py:125
  617.4 17.3 %collective-permute-start.24 = (bf16[32,1603]{0,1:T(8,128)(2,1)S(1)}, bf16[32,1603]{0,1:T(8,128)(2,1)S(1)}, u32[]{:S(2)}, u32[]{:S(2)}) collective-permute-start(bf16[32,1603]{0,1:T(8,128)(2,1)S(1)} %get-tuple-element.800), channel_id=1, source_target_pairs={{0,1},{1,2},{2,3},{3,0},{4,5},{5,6},{6,7},{7,4},{8,9},{9,10},{10,1... | collective-permute-start | bytes 307784 | tf_op jit(solution)/shard_map/ppermute | solution.py:241
  622.2 30.2 %collective-permute-start.25 = (bf16[32,1603]{0,1:T(8,128)(2,1)S(1)}, bf16[32,1603]{0,1:T(8,128)(2,1)S(1)}, u32[]{:S(2)}, u32[]{:S(2)}) collective-permute-start(bf16[32,1603]{0,1:T(8,128)(2,1)S(1)} %get-tuple-element.802), channel_id=1, source_target_pairs={{0,2},{1,3},{2,0},{3,1},{4,6},{5,7},{6,4},{7,5},{8,10},{9,11},{10,... | collective-permute-start | bytes 307784 | tf_op jit(solution)/shard_map/ppermute | solution.py:241
  624.8 27.5 %collective-permute-start.26 = (bf16[32,1603]{0,1:T(8,128)(2,1)S(1)}, bf16[32,1603]{0,1:T(8,128)(2,1)S(1)}, u32[]{:S(2)}, u32[]{:S(2)}) collective-permute-start(bf16[32,1603]{0,1:T(8,128)(2,1)S(1)} %get-tuple-element.801), channel_id=1, source_target_pairs={{0,3},{1,0},{2,1},{3,2},{4,7},{5,4},{6,5},{7,6},{8,11},{9,8},{10,9... | collective-permute-start | bytes 307784 | tf_op jit(solution)/shard_map/ppermute | solution.py:241
  634.7 30.9 %collective-permute-start.59 = (bf16[640,512]{1,0:T(8,128)(2,1)S(1)}, bf16[640,512]{1,0:T(8,128)(2,1)S(1)}, u32[]{:S(2)}, u32[]{:S(2)}) collective-permute-start(bf16[640,512]{1,0:T(8,128)(2,1)S(1)} %fusion.231), channel_id=1, source_target_pairs={{0,1},{1,2},{2,3},{3,0},{4,5},{5,6},{6,7},{7,4},{8,9},{9,10},{10,1... | collective-permute-start | bytes 1966088 | tf_op jit(solution)/shard_map/ppermute | solution.py:266
  656.7 45.2 %collective-permute-start.40 = (bf16[256,2560]{1,0:T(8,128)(2,1)S(1)}, bf16[256,2560]{1,0:T(8,128)(2,1)S(1)}, u32[]{:S(2)}, u32[]{:S(2)}) collective-permute-start(bf16[256,2560]{1,0:T(8,128)(2,1)S(1)} %slice.502), channel_id=1, source_target_pairs={{0,8},{4,12},{8,0},{12,4},{16,24},{20,28},{24,16},{28,20},{1,9},{5... | collective-permute-start | bytes 3932168 | tf_op jit(solution)/shard_map/ppermute | solution.py:125
  664.1 37.3 %collective-permute-start.28 = (bf16[64,1603]{0,1:T(8,128)(2,1)S(1)}, bf16[64,1603]{0,1:T(8,128)(2,1)S(1)}, u32[]{:S(2)}, u32[]{:S(2)}) collective-permute-start(bf16[64,1603]{0,1:T(8,128)(2,1)S(1)} %pad_maximum_fusion.36), channel_id=1, source_target_pairs={{0,8},{4,12},{8,0},{12,4},{16,24},{20,28},{24,16},{28,20},{1,9},{5... | collective-permute-start | bytes 615560 | tf_op jit(solution)/shard_map/ppermute | solution.py:125
  665.8 47.7 %collective-permute-start.60 = (bf16[640,512]{1,0:T(8,128)(2,1)S(1)}, bf16[640,512]{1,0:T(8,128)(2,1)S(1)}, u32[]{:S(2)}, u32[]{:S(2)}) collective-permute-start(bf16[640,512]{1,0:T(8,128)(2,1)S(1)} %fusion.230), channel_id=1, source_target_pairs={{0,1},{1,2},{2,3},{3,0},{4,5},{5,6},{6,7},{7,4},{8,9},{9,10},{10,1... | collective-permute-start | bytes 1966088 | tf_op jit(solution)/shard_map/ppermute | solution.py:266
  700.8 17.0 %collective-permute-start.50 = (bf16[128,2560]{1,0:T(8,128)(2,1)S(1)}, bf16[128,2560]{1,0:T(8,128)(2,1)S(1)}, u32[]{:S(2)}, u32[]{:S(2)}) collective-permute-start(bf16[128,2560]{1,0:T(8,128)(2,1)S(1)} %slice.514), channel_id=1, source_target_pairs={{0,8},{4,12},{8,0},{12,4},{16,24},{20,28},{24,16},{28,20},{1,9},{5... | collective-permute-start | bytes 1966088 | tf_op jit(solution)/shard_map/ppermute | solution.py:125
  702.3 45.8 %collective-permute-start.41 = (bf16[128,2560]{1,0:T(8,128)(2,1)S(1)}, bf16[128,2560]{1,0:T(8,128)(2,1)S(1)}, u32[]{:S(2)}, u32[]{:S(2)}) collective-permute-start(bf16[128,2560]{1,0:T(8,128)(2,1)S(1)} %slice.504), channel_id=1, source_target_pairs={{0,16},{4,20},{8,24},{12,28},{16,0},{20,4},{24,8},{28,12},{1,17},{... | collective-permute-start | bytes 1966088 | tf_op jit(solution)/shard_map/ppermute | solution.py:125
  713.7 58.8 %collective-permute-start.61 = (bf16[640,256]{1,0:T(8,128)(2,1)S(1)}, bf16[640,256]{1,0:T(8,128)(2,1)S(1)}, u32[]{:S(2)}, u32[]{:S(2)}) collective-permute-start(bf16[640,256]{1,0:T(8,128)(2,1)S(1)} %slice.522), channel_id=1, source_target_pairs={{0,8},{4,12},{8,0},{12,4},{16,24},{20,28},{24,16},{28,20},{1,9},{5... | collective-permute-start | bytes 983048 | tf_op jit(solution)/shard_map/ppermute | solution.py:125
  718.1 32.2 %collective-permute-start.51 = (bf16[32,2560]{1,0:T(8,128)(2,1)S(1)}, bf16[32,2560]{1,0:T(8,128)(2,1)S(1)}, u32[]{:S(2)}, u32[]{:S(2)}) collective-permute-start(bf16[32,2560]{1,0:T(8,128)(2,1)S(1)} %get-tuple-element.788), channel_id=1, source_target_pairs={{0,1},{1,2},{2,3},{3,0},{4,5},{5,6},{6,7},{7,4},{8,9},{9,10},{10,1... | collective-permute-start | bytes 491528 | tf_op jit(solution)/shard_map/ppermute | solution.py:241
  745.7 16.5 %collective-permute-start.52 = (bf16[32,2560]{1,0:T(8,128)(2,1)S(1)}, bf16[32,2560]{1,0:T(8,128)(2,1)S(1)}, u32[]{:S(2)}, u32[]{:S(2)}) collective-permute-start(bf16[32,2560]{1,0:T(8,128)(2,1)S(1)} %get-tuple-element.790), channel_id=1, source_target_pairs={{0,2},{1,3},{2,0},{3,1},{4,6},{5,7},{6,4},{7,5},{8,10},{9,11},{10,... | collective-permute-start | bytes 491528 | tf_op jit(solution)/shard_map/ppermute | solution.py:241
  745.7 23.2 %collective-permute-start.53 = (bf16[32,2560]{1,0:T(8,128)(2,1)S(1)}, bf16[32,2560]{1,0:T(8,128)(2,1)S(1)}, u32[]{:S(2)}, u32[]{:S(2)}) collective-permute-start(bf16[32,2560]{1,0:T(8,128)(2,1)S(1)} %get-tuple-element.789), channel_id=1, source_target_pairs={{0,3},{1,0},{2,1},{3,2},{4,7},{5,4},{6,5},{7,6},{8,11},{9,8},{10,9... | collective-permute-start | bytes 491528 | tf_op jit(solution)/shard_map/ppermute | solution.py:241
  748.3 22.2 %collective-permute-start.42 = (bf16[32,2560]{1,0:T(8,128)(2,1)S(1)}, bf16[32,2560]{1,0:T(8,128)(2,1)S(1)}, u32[]{:S(2)}, u32[]{:S(2)}) collective-permute-start(bf16[32,2560]{1,0:T(8,128)(2,1)S(1)} %get-tuple-element.791), channel_id=1, source_target_pairs={{0,1},{1,2},{2,3},{3,0},{4,5},{5,6},{6,7},{7,4},{8,9},{9,10},{10,1... | collective-permute-start | bytes 491528 | tf_op jit(solution)/shard_map/ppermute | solution.py:241
  750.3 20.2 %collective-permute-start.43 = (bf16[32,2560]{1,0:T(8,128)(2,1)S(1)}, bf16[32,2560]{1,0:T(8,128)(2,1)S(1)}, u32[]{:S(2)}, u32[]{:S(2)}) collective-permute-start(bf16[32,2560]{1,0:T(8,128)(2,1)S(1)} %get-tuple-element.793), channel_id=1, source_target_pairs={{0,2},{1,3},{2,0},{3,1},{4,6},{5,7},{6,4},{7,5},{8,10},{9,11},{10,... | collective-permute-start | bytes 491528 | tf_op jit(solution)/shard_map/ppermute | solution.py:241
  774.4 14.4 %collective-permute-start.55 = (bf16[64,2560]{1,0:T(8,128)(2,1)S(1)}, bf16[64,2560]{1,0:T(8,128)(2,1)S(1)}, u32[]{:S(2)}, u32[]{:S(2)}) collective-permute-start(bf16[64,2560]{1,0:T(8,128)(2,1)S(1)} %pad_maximum_fusion.42), channel_id=1, source_target_pairs={{0,16},{4,20},{8,24},{12,28},{16,0},{20,4},{24,8},{28,12},{1,17},{... | collective-permute-start | bytes 983048 | tf_op jit(solution)/shard_map/ppermute | solution.py:125
  (253 other events, 1724.2 us)

commit v2 on v1

--- a/solution.py
+++ b/solution.py
@@ -3,6 +3,8 @@
 import jax
 import jax.numpy as jnp
 from jax import lax
+from jax.experimental import pallas as pl
+from jax.experimental.pallas import tpu as pltpu
 from jax.sharding import PartitionSpec as P
 
 HD = 64
@@ -28,21 +30,15 @@
 
 
 def rotate(values, cosine_tab, sine_tab):
-    half = values.shape[-1] // 2
-    first = values[..., :half]
-    second = values[..., half:]
-    return jnp.concatenate(
-        [first * cosine_tab - second * sine_tab, second * cosine_tab + first * sine_tab], -1
-    )
+    heads = values.reshape(-1, 2, HD // 2, values.shape[-1])
+    first, second = (heads[:, 0], heads[:, 1])
+    return jnp.stack(
+        [first * cosine_tab - second * sine_tab, second * cosine_tab + first * sine_tab], 1
+    ).reshape(values.shape)
 
 
 def unrotate(grads, cosine_tab, sine_tab):
-    half = grads.shape[-1] // 2
-    first = grads[..., :half]
-    second = grads[..., half:]
-    return jnp.concatenate(
-        [first * cosine_tab + second * sine_tab, second * cosine_tab - first * sine_tab], -1
-    )
+    return rotate(grads, cosine_tab, -sine_tab)
 
 
 def doc_tables(positions, doc_lengths):
@@ -53,71 +49,185 @@
     return (doc_index, positions - offset)
 
 
-def head_scores(query_grp, key_grp, allowed):
-    scores = jnp.einsum(
-        "qgd,td->gqt", query_grp, key_grp, preferred_element_type=jnp.float32
-    ) * HD ** (-0.5)
-    return jnp.where(allowed[None], scores, -1e30)
-
-
-def attend_head(query_grp, key_grp, value_grp, allowed):
-    scores = head_scores(query_grp, key_grp, allowed)
-    peak = jnp.max(scores, axis=-1, keepdims=True)
-    weights = jnp.exp(scores - peak)
-    total = jnp.sum(weights, axis=-1, keepdims=True)
-    probs = (weights / total).astype(jnp.bfloat16)
-    output = jnp.einsum("gqt,td->qgd", probs, value_grp, preferred_element_type=jnp.float32)
-    return (output, peak[..., 0] + jnp.log(total[..., 0]))
-
-
-def attend_back(query_grp, key_grp, value_grp, allowed, log_total, grad_out):
-    scores = head_scores(query_grp, key_grp, allowed)
-    probs_full = jnp.exp(scores - log_total[..., None])
-    probs = probs_full.astype(jnp.bfloat16)
-    grad_probs = jnp.einsum("qgd,td->gqt", grad_out, value_grp, preferred_element_type=jnp.float32)
-    grad_value = jnp.einsum("gqt,qgd->td", probs, grad_out, preferred_element_type=jnp.float32)
-    delta = jnp.sum(probs_full * grad_probs, axis=-1, keepdims=True)
-    grad_scores = (probs_full * (grad_probs - delta)).astype(jnp.bfloat16)
-    grad_query = jnp.einsum(
-        "gqt,td->qgd", grad_scores, key_grp, preferred_element_type=jnp.float32
-    ) * HD ** (-0.5)
-    grad_key = jnp.einsum(
-        "gqt,qgd->td", grad_scores, query_grp, preferred_element_type=jnp.float32
-    ) * HD ** (-0.5)
-    return (grad_query, grad_key, grad_value)
-
-
-def stack_heads(queries, keys_all, values_all):
-    rows = queries.shape[0]
-    kv_heads = keys_all.shape[1] // HD
-    query_stack = queries.reshape(rows, kv_heads, -1, HD).transpose(1, 0, 2, 3)
-    key_stack = keys_all.reshape(-1, kv_heads, HD).transpose(1, 0, 2)
-    value_stack = values_all.reshape(-1, kv_heads, HD).transpose(1, 0, 2)
-    return (query_stack, key_stack, value_stack)
-
-
-def attention_forward(queries, keys_all, values_all, allowed):
-    rows = queries.shape[0]
-    stacks = stack_heads(queries, keys_all, values_all)
-    outputs, log_total = lax.map(
-        lambda group: attend_head(group[0], group[1], group[2], allowed), stacks
-    )
-    return (outputs.transpose(1, 0, 2, 3).reshape(rows, -1), log_total)
-
-
-def attention_backward(queries, keys_all, values_all, allowed, log_total, grad_out):
-    rows = queries.shape[0]
-    kv_heads = keys_all.shape[1] // HD
-    query_stack, key_stack, value_stack = stack_heads(queries, keys_all, values_all)
-    grad_stack = grad_out.reshape(rows, kv_heads, -1, HD).transpose(1, 0, 2, 3)
-    grad_query, grad_key, grad_value = lax.map(
-        lambda group: attend_back(group[0], group[1], group[2], allowed, group[3], group[4]),
-        (query_stack, key_stack, value_stack, log_total, grad_stack),
-    )
-    grad_query = grad_query.transpose(1, 0, 2, 3).reshape(rows, -1)
-    grad_key = grad_key.transpose(1, 0, 2).reshape(-1, keys_all.shape[1])
-    grad_value = grad_value.transpose(1, 0, 2).reshape(-1, keys_all.shape[1])
-    return (grad_query, grad_key, grad_value)
+def tile_bias(base, tile, low_key, positions, active):
+    rows = active.shape[0]
+    keys = base + tile * rows + lax.broadcasted_iota(jnp.int32, (rows, positions.shape[1]), 0)
+    own = keys == positions
+    seen = (keys >= low_key) & (keys <= positions) & ((active > 0) | own)
+    return jnp.where(seen, 0.0, -1e30)
+
+
+def attend_kernel(places, low_ref, act_ref, query_ref, k0, k1, k2, k3, v0, v1, v2, v3,
+                  out_ref, log_ref, bias_ref, key_ref, value_ref, top_ref, sum_ref, acc_ref):
+    rows = k0.shape[1]
+    heads = query_ref.shape[0] // HD
+    first_tile = places[1]
+    @pl.when(pl.program_id(0) == 0)
+    def _():
+        positions = places[0] + lax.broadcasted_iota(jnp.int32, (1, rows), 1)
+        for tile in range(REACH + 1):
+            @pl.when(tile >= first_tile)
+            def _(tile=tile):
+                bias_ref[tile] = tile_bias(places[0] - REACH * rows, tile, low_ref[...], positions,
+                                           act_ref[tile * rows:(tile + 1) * rows, :])
+    even = places[2] == 0
+    key_ref[3] = k0[...]
+    value_ref[3] = v0[...]
+    key_ref[2] = jnp.where(even, k3[...], k1[...])
+    value_ref[2] = jnp.where(even, v3[...], v1[...])
+    key_ref[1] = k2[...]
+    value_ref[1] = v2[...]
+    key_ref[0] = jnp.where(even, k1[...], k3[...])
+    value_ref[0] = jnp.where(even, v1[...], v3[...])
+    query = query_ref[...] * jnp.bfloat16(HD ** (-0.5))
+    query = jnp.concatenate([query[i * HD:(i + 1) * HD] for i in range(heads)], 1)
+
+    def scores(tile):
+        s = lax.dot_general(key_ref[tile], query, (((0,), (0,)), ((), ())), preferred_element_type=jnp.float32)
+        bias = bias_ref[tile]
+        return s + jnp.concatenate([bias] * heads, 1)
+
+    s = scores(REACH)
+    top = jnp.max(s, axis=0, keepdims=True)
+    p = jnp.exp(s - top)
+    top_ref[...] = top
+    sum_ref[...] = jnp.sum(p, axis=0, keepdims=True)
+    acc_ref[...] = jnp.dot(value_ref[REACH], p.astype(jnp.bfloat16), preferred_element_type=jnp.float32)
+
+    def body(tile, carry):
+        s = scores(tile)
+        old = top_ref[...]
+        top = jnp.maximum(old, jnp.max(s, axis=0, keepdims=True))
+        p = jnp.exp(s - top)
+        keep = jnp.exp(old - top)
+        top_ref[...] = top
+        sum_ref[...] = sum_ref[...] * keep + jnp.sum(p, axis=0, keepdims=True)
+        acc_ref[...] = acc_ref[...] * keep + jnp.dot(value_ref[tile], p.astype(jnp.bfloat16), preferred_element_type=jnp.float32)
+        return carry
+    lax.fori_loop(first_tile, REACH, body, 0)
+    total = sum_ref[...]
+    out = (acc_ref[...] / total).astype(jnp.bfloat16)
+    for i in range(heads):
+        out_ref[i * HD:(i + 1) * HD, :] = out[:, i * rows:(i + 1) * rows]
+    log_ref[0] = top_ref[...] + jnp.log(total)
+
+
+def pair_specs(rows, heads):
+    keys = pl.BlockSpec((HD, rows), lambda h, places: (h, 0))
+    values = pl.BlockSpec((HD, rows), lambda h, places: (heads + h, 0))
+    return [keys] * 4 + [values] * 4
+
+
+def attend(places, low_key, active, query, pairs):
+    width, rows = query.shape
+    heads = pairs[0].shape[0] // (2 * HD)
+    group = width // heads
+    wide = group // HD * rows
+    whole = lambda h, places: (0, 0)
+    return pl.pallas_call(
+        attend_kernel,
+        out_shape=(jax.ShapeDtypeStruct((width, rows), jnp.bfloat16),
+                   jax.ShapeDtypeStruct((heads, 1, wide), jnp.float32)),
+        grid_spec=pltpu.PrefetchScalarGridSpec(
+            num_scalar_prefetch=1, grid=(heads,),
+            in_specs=[pl.BlockSpec((1, rows), whole), pl.BlockSpec((4 * rows, 1), whole),
+                      pl.BlockSpec((group, rows), lambda h, places: (h, 0))] + pair_specs(rows, heads),
+            out_specs=(pl.BlockSpec((group, rows), lambda h, places: (h, 0)),
+                       pl.BlockSpec((1, 1, wide), lambda h, places: (h, 0, 0))),
+            scratch_shapes=[pltpu.VMEM((4, rows, rows), jnp.float32),
+                            pltpu.VMEM((4, HD, rows), jnp.bfloat16),
+                            pltpu.VMEM((4, HD, rows), jnp.bfloat16),
+                            pltpu.VMEM((1, wide), jnp.float32),
+                            pltpu.VMEM((1, wide), jnp.float32),
+                            pltpu.VMEM((HD, wide), jnp.float32)]),
+        cost_estimate=pl.CostEstimate(flops=4 * width * rows * rows * 16, bytes_accessed=4 * width * rows * 2, transcendentals=0),
+        name="attend",
+    )(places, low_key, active, query, *pairs, *pairs)
+
+
+def attend_back_kernel(places, low_ref, act_ref, query_ref, out_ref, grad_ref, log_ref, k0, k1, k2, k3, v0, v1, v2, v3,
+                       dq_ref, own_ref, prev_ref, bias_ref, key_ref, value_ref, acc_ref):
+    rows = k0.shape[1]
+    heads = query_ref.shape[0] // HD
+    first_tile = places[1]
+    @pl.when(pl.program_id(0) == 0)
+    def _():
+        positions = places[0] + lax.broadcasted_iota(jnp.int32, (1, rows), 1)
+        for tile in range(REACH + 1):
+            @pl.when(tile >= first_tile)
+            def _(tile=tile):
+                bias_ref[tile] = tile_bias(places[0] - REACH * rows, tile, low_ref[...], positions,
+                                           act_ref[tile * rows:(tile + 1) * rows, :])
+    even = places[2] == 0
+    key_ref[3] = k0[...]
+    value_ref[3] = v0[...]
+    key_ref[2] = jnp.where(even, k3[...], k1[...])
+    value_ref[2] = jnp.where(even, v3[...], v1[...])
+    key_ref[1] = k2[...]
+    value_ref[1] = v2[...]
+    key_ref[0] = jnp.where(even, k1[...], k3[...])
+    value_ref[0] = jnp.where(even, v1[...], v3[...])
+    spread = lambda x: jnp.concatenate([x[i * HD:(i + 1) * HD] for i in range(heads)], 1)
+    query = spread(query_ref[...] * jnp.bfloat16(HD ** (-0.5)))
+    grad = spread(grad_ref[...])
+    delta = jnp.sum(grad.astype(jnp.float32) * spread(out_ref[...]).astype(jnp.float32), axis=0, keepdims=True)
+    logs = log_ref[0]
+    acc_ref[...] = jnp.zeros_like(acc_ref)
+
+    def step(tile):
+        s = lax.dot_general(key_ref[tile], query, (((0,), (0,)), ((), ())), preferred_element_type=jnp.float32)
+        bias = bias_ref[tile]
+        p = jnp.exp(s + jnp.concatenate([bias] * heads, 1) - logs)
+        dp = lax.dot_general(value_ref[tile], grad, (((0,), (0,)), ((), ())), preferred_element_type=jnp.float32)
+        ds = (p * (dp - delta)).astype(jnp.bfloat16)
+        acc_ref[...] += jnp.dot(key_ref[tile], ds, preferred_element_type=jnp.float32)
+        dk = lax.dot_general(query, ds, (((1,), (1,)), ((), ())), preferred_element_type=jnp.float32)
+        dv = lax.dot_general(grad, p.astype(jnp.bfloat16), (((1,), (1,)), ((), ())), preferred_element_type=jnp.float32)
+        return dk, dv
+
+    dk, dv = step(REACH)
+    own_ref[0] = dk
+    own_ref[1] = dv
+    prev_ref[...] = jnp.zeros_like(prev_ref)
+
+    def body(tile, carry):
+        dk, dv = step(tile)
+        slot = jnp.where(even, tile, REACH - 1 - tile)
+        prev_ref[slot, 0] = dk.astype(jnp.bfloat16)
+        prev_ref[slot, 1] = dv.astype(jnp.bfloat16)
+        return carry
+    lax.fori_loop(first_tile, REACH, body, 0)
+    dq = acc_ref[...] * (HD ** (-0.5))
+    for i in range(heads):
+        dq_ref[i * HD:(i + 1) * HD, :] = dq[:, i * rows:(i + 1) * rows]
+
+
+def attend_back(places, low_key, active, query, out, grad, logs, pairs):
+    width, rows = query.shape
+    heads = pairs[0].shape[0] // (2 * HD)
+    group = width // heads
+    wide = group // HD * rows
+    whole = lambda h, places: (0, 0)
+    mine = pl.BlockSpec((group, rows), lambda h, places: (h, 0))
+    own = pl.BlockSpec((2, HD, rows), lambda h, places: (0, h, 0))
+    prev = pl.BlockSpec((REACH, 2, HD, rows), lambda h, places: (0, 0, h, 0))
+    return pl.pallas_call(
+        attend_back_kernel,
+        out_shape=(jax.ShapeDtypeStruct((width, rows), jnp.float32),
+                   jax.ShapeDtypeStruct((2, heads * HD, rows), jnp.float32),
+                   jax.ShapeDtypeStruct((REACH, 2, heads * HD, rows), jnp.bfloat16)),
+        grid_spec=pltpu.PrefetchScalarGridSpec(
+            num_scalar_prefetch=1, grid=(heads,),
+            in_specs=[pl.BlockSpec((1, rows), whole), pl.BlockSpec((4 * rows, 1), whole),
+                      mine, mine, mine, pl.BlockSpec((1, 1, wide), lambda h, places: (h, 0, 0))] + pair_specs(rows, heads),
+            out_specs=(mine, own, prev),
+            scratch_shapes=[pltpu.VMEM((4, rows, rows), jnp.float32),
+                            pltpu.VMEM((4, HD, rows), jnp.bfloat16),
+                            pltpu.VMEM((4, HD, rows), jnp.bfloat16),
+                            pltpu.VMEM((HD, wide), jnp.float32)]),
+        cost_estimate=pl.CostEstimate(flops=10 * width * rows * rows * 16, bytes_accessed=8 * width * rows * 2, transcendentals=0),
+        name="attend_back",
+    )(places, low_key, active, query, out, grad, logs, *pairs, *pairs)
 
 
 def swap(block, mask):
@@ -134,23 +244,16 @@
 
 def halo(block):
     devices = range(lax.axis_size("seq"))
-    even = lax.axis_index("seq") % 2 == 0
     two = moved(block, [i + 2 for i in devices])
     mixed = moved(block, [i + 1 if i % 2 == 0 else i + 3 for i in devices])
-    across = swap(two, 1)
-    return (jnp.where(even, mixed, across), two, jnp.where(even, across, mixed))
-
-
-def halo_back(third, second, first):
+    return (mixed, two, swap(two, 1))
+
+
+def halo_back(mixed, second, across):
     devices = range(lax.axis_size("seq"))
-    even = lax.axis_index("seq") % 2 == 0
-    across = swap(jnp.where(even, first, third).astype(jnp.bfloat16), 1)
-    mixed = moved(
-        jnp.where(even, third, first).astype(jnp.bfloat16),
-        [i - 1 if i % 2 == 1 else i - 3 for i in devices],
-    )
-    both = (second + across.astype(jnp.float32)).astype(jnp.bfloat16)
-    two = moved(both, [i - 2 for i in devices])
+    across = swap(across, 1)
+    mixed = moved(mixed, [i - 1 if i % 2 == 1 else i - 3 for i in devices])
+    two = moved(added(second, across), [i - 2 for i in devices])
     return two.astype(jnp.float32) + mixed.astype(jnp.float32)
 
 
@@ -303,23 +406,29 @@
     key_width = w_key.shape[1]
     seq_index = lax.axis_index("seq")
     local_pos = seq_index * rows + jnp.arange(rows, dtype=jnp.int32)
-    key_pos = (seq_index - REACH) * rows + jnp.arange((REACH + 1) * rows, dtype=jnp.int32)
     doc_lengths = lengths[0]
-    query_doc, place = doc_tables(local_pos, doc_lengths)
-    key_doc, unused_place = doc_tables(key_pos, doc_lengths)
-    base_mask = (
-        (key_pos[None, :] >= 0)
-        & (key_pos[None, :] <= local_pos[:, None])
-        & (key_doc[None, :] == query_doc[:, None])
-    )
-    own_key = key_pos[None, :] == local_pos[:, None]
+    unused_doc, place = doc_tables(local_pos, doc_lengths)
+    low_key = (local_pos - place)[None, :]
+    window = (seq_index - REACH) * rows
+    first_tile = jnp.maximum((low_key[0, 0] - window) // rows, 0)
+    even = seq_index % 2
+    places = jnp.stack([seq_index * rows, first_tile, even]).astype(jnp.int32)
     half = HD // 2
     freqs = jnp.exp(-math.log(10000.0) * 2.0 * jnp.arange(half, dtype=jnp.float32) / HD)
-    angles = place.astype(jnp.float32)[:, None, None] * freqs[None, None, :]
+    angles = freqs[:, None] * place.astype(jnp.float32)[None, :]
     cosine_tab = jnp.cos(angles)
     sine_tab = jnp.sin(angles)
     depth_row = depth[0]
-    depth_all = jnp.concatenate([*halo(depth_row), depth_row], 0)
+    mixed_depth, two_depth, across_depth = halo(depth_row)
+    depth_all = jnp.concatenate(
+        [
+            jnp.where(even == 0, mixed_depth, across_depth),
+            two_depth,
+            jnp.where(even == 0, across_depth, mixed_depth),
+            depth_row,
+        ],
+        0,
+    )
     router_rows = router.astype(jnp.float32)
     order_a, order_b = bit_orders()
     spread_a = row_spread(width, order_a)
@@ -331,24 +440,14 @@
         normed_low = normed.astype(jnp.bfloat16)
         key_pre = jnp.dot(normed_low, w_key, preferred_element_type=jnp.float32)
         value_low = low_dot(normed_low, w_value)
-        key_low = (
-            rotate(key_pre.reshape(rows, -1, HD), cosine_tab, sine_tab)
-            .reshape(rows, -1)
-            .astype(jnp.bfloat16)
-        )
-        local_pair = jnp.concatenate([key_low, value_low], 1)
-        pair = jnp.concatenate([*halo(local_pair), local_pair], 0)
+        key_low = rotate(key_pre.T, cosine_tab, sine_tab).astype(jnp.bfloat16)
+        local_pair = jnp.concatenate([key_low, value_low.T], 0)
+        pairs = (local_pair, *halo(local_pair))
         query_pre = jnp.dot(normed_low, w_query, preferred_element_type=jnp.float32)
-        query_low = (
-            rotate(query_pre.reshape(rows, -1, HD), cosine_tab, sine_tab)
-            .reshape(rows, -1)
-            .astype(jnp.bfloat16)
-        )
-        keys_all = pair[:, :key_width]
-        values_all = pair[:, key_width:]
-        allowed = base_mask & ((depth_all > level)[None, :] | own_key)
-        attended, log_total = attention_forward(query_low, keys_all, values_all, allowed)
-        attended_low = attended.astype(jnp.bfloat16)
+        query_low = rotate(query_pre.T, cosine_tab, sine_tab).astype(jnp.bfloat16)
+        activity = (depth_all > level).astype(jnp.int32)[:, None]
+        attended, log_total = attend(places, low_key, activity, query_low, pairs)
+        attended_low = attended.T
         attn_out = jnp.dot(attended_low, w_out, preferred_element_type=jnp.float32)
         mid_state = state + attn_out
         normed2, inverse2 = rms_forward(mid_state, norm2_gain)
@@ -368,9 +467,9 @@
                 inverse1,
                 normed_low,
                 query_low,
-                keys_all,
-                values_all,
-                allowed,
+                pairs,
+                activity,
+                attended,
                 log_total,
                 attended_low,
                 mid_state,
@@ -403,9 +502,9 @@
             inverse1,
             normed_low,
             query_low,
-            keys_all,
-            values_all,
-            allowed,
+            pairs,
+            activity,
+            attended,
             log_total,
             attended_low,
             mid_state,
@@ -451,24 +550,16 @@
         grad_attended = jnp.einsum(
             "te,de->td", grad_attn, w_out, preferred_element_type=jnp.float32
         ).astype(jnp.bfloat16)
-        grad_query, grad_keys, grad_values = attention_backward(
-            query_low, keys_all, values_all, allowed, log_total, grad_attended
-        )
-        grad_pair = jnp.concatenate([grad_keys, grad_values], 1)
-        local_pair = grad_pair[REACH * rows :] + halo_back(
-            grad_pair[:rows], grad_pair[rows : 2 * rows], grad_pair[2 * rows : 3 * rows]
-        )
-        grad_query_pre = (
-            unrotate(grad_query.reshape(rows, -1, HD), cosine_tab, sine_tab)
-            .reshape(rows, -1)
-            .astype(jnp.bfloat16)
-        )
+        grad_query, own_pair, prior = attend_back(
+            places, low_key, activity, query_low, attended, grad_attended.T, log_total, pairs
+        )
+        prior = prior.reshape(REACH, -1, rows)
+        local_pair = own_pair.reshape(-1, rows) + halo_back(prior[0], prior[1], prior[2])
+        grad_query_pre = unrotate(grad_query, cosine_tab, sine_tab).astype(jnp.bfloat16).T
         grad_key_pre = (
-            unrotate(local_pair[:, :key_width].reshape(rows, -1, HD), cosine_tab, sine_tab)
-            .reshape(rows, -1)
-            .astype(jnp.bfloat16)
-        )
-        grad_value_pre = local_pair[:, key_width:].astype(jnp.bfloat16)
+            unrotate(local_pair[:key_width], cosine_tab, sine_tab).astype(jnp.bfloat16).T
+        )
+        grad_value_pre = local_pair[key_width:].astype(jnp.bfloat16).T
         router_term = (grad_logit / inverse1[:, 0])[:, None] * (
             jnp.arange(R)[None, :] == level
         ).astype(jnp.float32)

time: 822 us -> 617 us (0.75)
  matrix products: 321 us -> 137 us
  waiting for transfers between devices: 124 us -> 219 us
  other arithmetic: 130 us -> 58.9 us
  starting transfers between devices: 178 us -> 117 us
  Pallas kernels: 0 us -> 44 us
  local copies, waits for them, and re-layouts: 51.7 us -> 30.4 us
    dot_general x105 -> x0, matrix products: 192 us -> none  [the longest x30 55.7 us: head_scores(): jnp.einsum('qgd,td->gqt', query_grp, key_grp, preferred_element_type=jnp....]
    ppermute x12, waiting for transfers between devices: 30.1 us -> 81.4 us  [reduce_rows(): lax.ppermute(part[distance * slots:(distance + 1) * slots], 'str', route)]
    ppermute x3, starting transfers between devices: 52.6 us -> 2.53 us  [reduce_columns(): running = added(lax.ppermute(running, 'str', route), block(step + 2))]
    pallas_call x0 -> x6, Pallas kernels: none -> 44 us  [the longest x3 23.9 us: attend_back(): pl.pallas_call(attend_back_kernel, out_shape=(jax.ShapeDtypeStruct((width...]
    and x30 -> x0, other arithmetic: 32.3 us -> none  [per_device(): allowed = base_mask & ((depth_all > level)[None, :] | own_key)]
    ppermute x37, waiting for transfers between devices: 52.5 us -> 83.7 us  [swap(): return lax.ppermute(block, 'seq', [(i, i ^ mask) for i in devices])]
    ppermute x12, starting transfers between devices: 61.7 us -> 32.2 us  [reduce_rows(): lax.ppermute(part[distance * slots:(distance + 1) * slots], 'str', route)]
    ppermute x14, waiting for transfers between devices: 33.7 us -> 50.1 us  [moved(): lax.ppermute(block, 'seq', [(i, t) for i, t in enumerate(targets) if t in...]
  transfers between devices with their start and end apart: 66 -> 66, of which waited for: 24 -> 25; matrix products, arithmetic and copies ran while one was open for 14% -> 19% of each run, Pallas kernels for 0% -> 0%
where the time goes in v2:
time: 617 us; the launch traced here: 611 us
  waiting for transfers between devices  219 us (35%)
  matrix products  137 us (22%)
  starting transfers between devices  117 us (19%)
  other arithmetic  58.9 us (10%)
  Pallas kernels  44 us (7%)
  local copies, waits for them, and re-layouts  30.4 us (5%)
    ppermute x37, waiting for transfers between devices, swap(): return lax.ppermute(block, 'seq', [(i, i ^ mask) for i in devices])  83.7 us
    ppermute x12, waiting for transfers between devices, reduce_rows(): lax.ppermute(part[distance * slots:(distance + 1) * slots], 'str', route)  81.4 us
    ppermute x14, waiting for transfers between devices, moved(): lax.ppermute(block, 'seq', [(i, t) for i, t in enumerate(targets) if t in...  50.1 us
    ppermute x37, starting transfers between devices, swap(): return lax.ppermute(block, 'seq', [(i, i ^ mask) for i in devices])  43.8 us
    ppermute x14, starting transfers between devices, moved(): lax.ppermute(block, 'seq', [(i, t) for i, t in enumerate(targets) if t in...  38.1 us
    ppermute x12, starting transfers between devices, reduce_rows(): lax.ppermute(part[distance * slots:(distance + 1) * slots], 'str', route)  32.2 us
    pallas_call x3, Pallas kernels, attend_back(): pl.pallas_call(attend_back_kernel, out_shape=(jax.ShapeDtypeStruct((width...  23.9 us
    dot_general x10, matrix products, outer(): jnp.einsum('tm,tn->mn', left, right, preferred_element_type=jnp.float32)  23.6 us
  transfers between devices with their start and end apart: 66, of which 25 were waited for; matrix products, arithmetic and copies ran while one was open for 19% of the time, Pallas kernels for 0%

profile of v2, /device:TPU:0, one launch (start us, length us, event | category | flops | bytes accessed | tf_op | source)
XLA Modules:
  0.0 610.7 jit_solution(9975432070477097340)
XLA Ops:
  3.8 4.7 collective-permute-start.1
  46.8 6.6 %attend.3 = (bf16[960,256]{1,0:T(8,128)(2,1)}, f32[5,1,768]{2,1,0:T(1,128)}) custom-call(s32[3]{0:T(128)} %pad_add_fusion.1.places, s32[1,256]{1,0:T(1,128)} %bitcast.344, s32[1024,1]{1,0:T(8,128)} %convert_element_type.577.act_ref, bf16[960,256]{1,0:T(8,128)(2,1)} %bitcast.312, bf16[640,256]{1,0:T(8,128)(2,1)} %pad_maximum_fusion.35.k0.v0, ...), custom_call_target="tpu_custom_call" | custom-call | flops 4026531840 | bytes 1966080 | tf_op jit(solution)/shard_map/attend/pallas_call | solution.py:127
  59.9 6.7 %multiply_convert_fusion.8 = (bf16[256,2560]{1,0:T(8,128)(2,1)S(1)}, f32[256,2560]{1,0:T(8,128)}) fusion(f32[256,2560]{1,0:T(8,128)S(1)} %fusion.222, bf16[256,960]{0,1:T(8,128)(2,1)S(1)} %multiply_convert_fusion.13, bf16[960,2560]{1,0:T(8,128)(2,1)} %param.25), kind=kOutput, calls=%fused_computation.38 | convolution fusion | flops 1262223360 | bytes 11960320 | tf_op jit(solution)/shard_map/dot_general | solution.py:456
  81.7 4.9 collective-permute-done.7.k2.v2
  91.2 6.6 %attend.4 = (bf16[960,256]{1,0:T(8,128)(2,1)}, f32[5,1,768]{2,1,0:T(1,128)}) custom-call(s32[3]{0:T(128)} %pad_add_fusion.1.places, s32[1,256]{1,0:T(1,128)} %bitcast.345, s32[1024,1]{1,0:T(8,128)} %convert_element_type.586.act_ref, bf16[960,256]{1,0:T(8,128)(2,1)} %bitcast.314, bf16[640,256]{1,0:T(8,128)(2,1)} %copy-done.95, bf16[640,256]{1,0:T(8,128)(2,1)} %copy-done.146, ...), custom_call_target="tpu_custom_call" | custom-call | flops 4026531840 | bytes 1966080 | tf_op jit(solution)/shard_map/attend/pallas_call | solution.py:127
  105.2 6.7 %multiply_convert_fusion.7 = (bf16[256,2560]{1,0:T(8,128)(2,1)S(1)}, f32[256,2560]{1,0:T(8,128)}) fusion(f32[256,2560]{1,0:T(8,128)S(1)} %fusion.224, bf16[256,960]{0,1:T(8,128)(2,1)S(1)} %multiply_convert_fusion.11, bf16[960,2560]{1,0:T(8,128)(2,1)} %param.25), kind=kOutput, calls=%fused_computation.36 | convolution fusion | flops 1262223360 | bytes 11960320 | tf_op jit(solution)/shard_map/dot_general | solution.py:456
  137.9 7.0 %attend.5 = (bf16[960,256]{1,0:T(8,128)(2,1)}, f32[5,1,768]{2,1,0:T(1,128)}) custom-call(s32[3]{0:T(128)} %pad_add_fusion.1.places, s32[1,256]{1,0:T(1,128)} %bitcast.346, s32[1024,1]{1,0:T(8,128)} %convert_element_type.594.act_ref, bf16[960,256]{1,0:T(8,128)(2,1)} %bitcast.316, bf16[640,256]{1,0:T(8,128)(2,1)} %copy-done.96, bf16[640,256]{1,0:T(8,128)(2,1)} %copy-done.149, ...), custom_call_target="tpu_custom_call" | custom-call | flops 4026531840 | bytes 1966080 | tf_op jit(solution)/shard_map/attend/pallas_call | solution.py:127
  171.2 8.1 %attend_back.3 = (f32[960,256]{1,0:T(8,128)}, f32[2,320,256]{2,1,0:T(8,128)}, bf16[3,2,320,256]{3,2,1,0:T(8,128)(2,1)}) custom-call(s32[3]{0:T(128)} %pad_add_fusion.1.places, s32[1,256]{1,0:T(1,128)} %bitcast.347, s32[1024,1]{1,0:T(8,128)} %convert_element_type.594.act_ref, bf16[960,256]{1,0:T(8,128)(2,1)} %bitcast.317, ...), custom_call_target="tpu_custom_call" | custom-call | flops 10066329600 | bytes 3932160 | tf_op jit(solution)/shard_map/attend_back/pallas_call | solution.py:214
  182.2 6.7 %collective-permute-start.12 = (bf16[640,256]{1,0:T(8,128)(2,1)S(1)}, bf16[640,256]{1,0:T(8,128)(2,1)S(1)}, u32[]{:S(2)}, u32[]{:S(2)}) collective-permute-start(bf16[640,256]{1,0:T(8,128)(2,1)S(1)} %bitcast.323), channel_id=1, source_target_pairs={{0,4},{4,0},{8,12},{12,8},{16,20},{20,16},{24,28},{28,24},{1,5},{5... | collective-permute-start | bytes 983048 | tf_op jit(solution)/shard_map/ppermute | solution.py:235
  195.3 9.3 %collective-permute-done.13 = bf16[640,256]{1,0:T(8,128)(2,1)S(1)} collective-permute-done((bf16[640,256]{1,0:T(8,128)(2,1)S(1)}, bf16[640,256]{1,0:T(8,128)(2,1)S(1)}, u32[]{:S(2)}, u32[]{:S(2)}) %collective-permute-start.13) | collective-permute-done | bytes 327712 | tf_op jit(solution)/shard_map/ppermute | solution.py:240
  218.0 7.9 %attend_back.4 = (f32[960,256]{1,0:T(8,128)}, f32[2,320,256]{2,1,0:T(8,128)}, bf16[3,2,320,256]{3,2,1,0:T(8,128)(2,1)}) custom-call(s32[3]{0:T(128)} %pad_add_fusion.1.places, s32[1,256]{1,0:T(1,128)} %bitcast.348, s32[1024,1]{1,0:T(8,128)} %convert_element_type.586.act_ref, bf16[960,256]{1,0:T(8,128)(2,1)} %bitcast.315, ...), custom_call_target="tpu_custom_call" | custom-call | flops 10066329600 | bytes 3932160 | tf_op jit(solution)/shard_map/attend_back/pallas_call | solution.py:214
  237.9 17.7 %collective-permute-done.16 = bf16[640,256]{1,0:T(8,128)(2,1)S(1)} collective-permute-done((bf16[640,256]{1,0:T(8,128)(2,1)S(1)}, bf16[640,256]{1,0:T(8,128)(2,1)S(1)}, u32[]{:S(2)}, u32[]{:S(2)}) %collective-permute-start.16) | collective-permute-done | bytes 327712 | tf_op jit(solution)/shard_map/ppermute | solution.py:240
  269.7 7.9 %attend_back.5 = (f32[960,256]{1,0:T(8,128)}, f32[2,320,256]{2,1,0:T(8,128)}, bf16[3,2,320,256]{3,2,1,0:T(8,128)(2,1)}) custom-call(s32[3]{0:T(128)} %pad_add_fusion.1.places, s32[1,256]{1,0:T(1,128)} %bitcast.349, s32[1024,1]{1,0:T(8,128)} %convert_element_type.577.act_ref, bf16[960,256]{1,0:T(8,128)(2,1)} %bitcast.313, ...), custom_call_target="tpu_custom_call" | custom-call | flops 10066329600 | bytes 3932160 | tf_op jit(solution)/shard_map/attend_back/pallas_call | solution.py:214
  300.8 15.2 %collective-permute-done.19 = bf16[640,256]{1,0:T(8,128)(2,1)S(1)} collective-permute-done((bf16[640,256]{1,0:T(8,128)(2,1)S(1)}, bf16[640,256]{1,0:T(8,128)(2,1)S(1)}, u32[]{:S(2)}, u32[]{:S(2)}) %collective-permute-start.19) | collective-permute-done | bytes 327712 | tf_op jit(solution)/shard_map/ppermute | solution.py:240
  317.3 6.1 collective-permute-start.31
  323.4 18.1 %maximum_maximum_fusion = bf16[768,1603]{0,1:T(8,128)(2,1)S(1)} fusion(bf16[256,3]{0,1:T(4,128)(2,1)S(1)} %multiply_convert_fusion.20, bf16[256,320]{0,1:T(8,128)(2,1)S(1)} %copy-done.67, bf16[256,320]{0,1:T(8,128)(2,1)S(1)} %bitcast.295, bf16[256,960]{0,1:T(8,128)(2,1)S(1)} %bitcast.289, bf16[256,3]{0,1:T(4,128)(2,1)S(1)} %multiply_convert_fusion.21, ...), kind=kLoop, calls=%fused_computation.40 | loop fusion | flops 29546496 | bytes 4924416 | tf_op jit(solution)/shard_map/concatenate | solution.py:386
  343.8 7.8 %collective-permute-done.32 = bf16[128,960]{0,1:T(8,128)(2,1)S(1)} collective-permute-done((bf16[128,960]{0,1:T(8,128)(2,1)S(1)}, bf16[128,960]{0,1:T(8,128)(2,1)S(1)}, u32[]{:S(2)}, u32[]{:S(2)}) %collective-permute-start.32) | collective-permute-done | bytes 245792 | tf_op jit(solution)/shard_map/ppermute | solution.py:235
  352.0 6.9 %collective-permute-start.35 = (bf16[32,960]{0,1:T(8,128)(2,1)S(1)}, bf16[32,960]{0,1:T(8,128)(2,1)S(1)}, u32[]{:S(2)}, u32[]{:S(2)}) collective-permute-start(bf16[32,960]{0,1:T(8,128)(2,1)S(1)} %get-tuple-element.183), channel_id=1, source_target_pairs={{0,3},{1,0},{2,1},{3,2},{4,7},{5,4},{6,5},{7,6},{8,11},{9,8},{10,9... | collective-permute-start | bytes 184328 | tf_op jit(solution)/shard_map/ppermute | solution.py:344
  358.9 16.5 %collective-permute-start.34 = (bf16[32,960]{0,1:T(8,128)(2,1)S(1)}, bf16[32,960]{0,1:T(8,128)(2,1)S(1)}, u32[]{:S(2)}, u32[]{:S(2)}) collective-permute-start(bf16[32,960]{0,1:T(8,128)(2,1)S(1)} %get-tuple-element.184), channel_id=1, source_target_pairs={{0,2},{1,3},{2,0},{3,1},{4,6},{5,7},{6,4},{7,5},{8,10},{9,11},{10,... | collective-permute-start | bytes 184328 | tf_op jit(solution)/shard_map/ppermute | solution.py:344
  378.3 18.6 %collective-permute-done.34 = bf16[32,960]{0,1:T(8,128)(2,1)S(1)} collective-permute-done((bf16[32,960]{0,1:T(8,128)(2,1)S(1)}, bf16[32,960]{0,1:T(8,128)(2,1)S(1)}, u32[]{:S(2)}, u32[]{:S(2)}) %collective-permute-start.34) | collective-permute-done | bytes 61472 | tf_op jit(solution)/shard_map/ppermute | solution.py:344
  397.7 7.8 %collective-permute-done.36 = bf16[32,960]{0,1:T(8,128)(2,1)S(1)} collective-permute-done((bf16[32,960]{0,1:T(8,128)(2,1)S(1)}, bf16[32,960]{0,1:T(8,128)(2,1)S(1)}, u32[]{:S(2)}, u32[]{:S(2)}) %collective-permute-start.36) | collective-permute-done | bytes 61472 | tf_op jit(solution)/shard_map/ppermute | solution.py:235
  407.5 5.8 collective-permute-done.37
  422.7 13.8 %collective-permute-done.22 = bf16[256,1603]{0,1:T(8,128)(2,1)S(1)} collective-permute-done((bf16[256,1603]{0,1:T(8,128)(2,1)S(1)}, bf16[256,1603]{0,1:T(8,128)(2,1)S(1)}, u32[]{:S(2)}, u32[]{:S(2)}) %collective-permute-start.22) | collective-permute-done | bytes 820768 | tf_op jit(solution)/shard_map/ppermute | solution.py:235
  441.2 6.1 %collective-permute-done.23 = bf16[128,1603]{0,1:T(8,128)(2,1)S(1)} collective-permute-done((bf16[128,1603]{0,1:T(8,128)(2,1)S(1)}, bf16[128,1603]{0,1:T(8,128)(2,1)S(1)}, u32[]{:S(2)}, u32[]{:S(2)}) %collective-permute-start.23) | collective-permute-done | bytes 410400 | tf_op jit(solution)/shard_map/ppermute | solution.py:235
  452.6 14.8 %collective-permute-done.26 = bf16[32,1603]{0,1:T(8,128)(2,1)S(1)} collective-permute-done((bf16[32,1603]{0,1:T(8,128)(2,1)S(1)}, bf16[32,1603]{0,1:T(8,128)(2,1)S(1)}, u32[]{:S(2)}, u32[]{:S(2)}) %collective-permute-start.26) | collective-permute-done | bytes 102624 | tf_op jit(solution)/shard_map/ppermute | solution.py:344
  469.1 24.7 %collective-permute-done.25 = bf16[32,1603]{0,1:T(8,128)(2,1)S(1)} collective-permute-done((bf16[32,1603]{0,1:T(8,128)(2,1)S(1)}, bf16[32,1603]{0,1:T(8,128)(2,1)S(1)}, u32[]{:S(2)}, u32[]{:S(2)}) %collective-permute-start.25) | collective-permute-done | bytes 102624 | tf_op jit(solution)/shard_map/ppermute | solution.py:344
  496.0 10.9 %collective-permute-done.27 = bf16[32,1603]{0,1:T(8,128)(2,1)S(1)} collective-permute-done((bf16[32,1603]{0,1:T(8,128)(2,1)S(1)}, bf16[32,1603]{0,1:T(8,128)(2,1)S(1)}, u32[]{:S(2)}, u32[]{:S(2)}) %collective-permute-start.27) | collective-permute-done | bytes 102624 | tf_op jit(solution)/shard_map/ppermute | solution.py:235
  510.0 7.9 %collective-permute-done.28 = bf16[64,1603]{0,1:T(8,128)(2,1)S(1)} collective-permute-done((bf16[64,1603]{0,1:T(8,128)(2,1)S(1)}, bf16[64,1603]{0,1:T(8,128)(2,1)S(1)}, u32[]{:S(2)}, u32[]{:S(2)}) %collective-permute-start.28) | collective-permute-done | bytes 205216 | tf_op jit(solution)/shard_map/ppermute | solution.py:235
  528.5 7.4 %collective-permute-done.50 = bf16[128,2560]{1,0:T(8,128)(2,1)S(1)} collective-permute-done((bf16[128,2560]{1,0:T(8,128)(2,1)S(1)}, bf16[128,2560]{1,0:T(8,128)(2,1)S(1)}, u32[]{:S(2)}, u32[]{:S(2)}) %collective-permute-start.50) | collective-permute-done | bytes 655392 | tf_op jit(solution)/shard_map/ppermute | solution.py:235
  544.3 10.0 %collective-permute-done.43 = bf16[32,2560]{1,0:T(8,128)(2,1)S(1)} collective-permute-done((bf16[32,2560]{1,0:T(8,128)(2,1)S(1)}, bf16[32,2560]{1,0:T(8,128)(2,1)S(1)}, u32[]{:S(2)}, u32[]{:S(2)}) %collective-permute-start.43) | collective-permute-done | bytes 163872 | tf_op jit(solution)/shard_map/ppermute | solution.py:344
  556.7 10.7 %collective-permute-done.52 = bf16[32,2560]{1,0:T(8,128)(2,1)S(1)} collective-permute-done((bf16[32,2560]{1,0:T(8,128)(2,1)S(1)}, bf16[32,2560]{1,0:T(8,128)(2,1)S(1)}, u32[]{:S(2)}, u32[]{:S(2)}) %collective-permute-start.52) | collective-permute-done | bytes 163872 | tf_op jit(solution)/shard_map/ppermute | solution.py:344
  592.2 5.0 collective-permute-done.64
  (745 shorter events, 290.8 us)
Async XLA Ops:
  0.7 40.2 %collective-permute-start = (s32[256]{0:T(256)}, s32[256]{0:T(256)}, u32[]{:S(2)}, u32[]{:S(2)}) collective-permute-start(s32[256]{0:T(256)} %bitcast.325), channel_id=1, source_target_pairs={{0,4},{4,16},{8,12},{12,24},{16,20},{24,28},{1,5},{5,17},{9,13},{1... | collective-permute-start | bytes 3080 | tf_op jit(solution)/shard_map/ppermute | solution.py:240
  3.8 35.4 %collective-permute-start.1 = (s32[256]{0:T(256)}, s32[256]{0:T(256)}, u32[]{:S(2)}, u32[]{:S(2)}) collective-permute-start(s32[256]{0:T(256)} %bitcast.326), channel_id=1, source_target_pairs={{0,8},{4,12},{8,16},{12,20},{16,24},{20,28},{1,9},{5,13},{9,17},{1... | collective-permute-start | bytes 3080 | tf_op jit(solution)/shard_map/ppermute | solution.py:240
  15.8 30.2 %collective-permute-start.3 = (bf16[640,256]{1,0:T(8,128)(2,1)}, bf16[640,256]{1,0:T(8,128)(2,1)}, u32[]{:S(2)}, u32[]{:S(2)}) collective-permute-start(bf16[640,256]{1,0:T(8,128)(2,1)} %pad_maximum_fusion.35.k0.v0), channel_id=1, source_target_pairs={{0,4},{4,16},{8,12},{12,24},{16,20},{24,28},{1,5},{5,17},{9,13},{1... | collective-permute-start | bytes 983048 | tf_op jit(solution)/shard_map/ppermute | solution.py:240
  19.4 22.1 %collective-permute-start.4 = (bf16[640,256]{1,0:T(8,128)(2,1)}, bf16[640,256]{1,0:T(8,128)(2,1)}, u32[]{:S(2)}, u32[]{:S(2)}) collective-permute-start(bf16[640,256]{1,0:T(8,128)(2,1)} %pad_maximum_fusion.35.k0.v0), channel_id=1, source_target_pairs={{0,8},{4,12},{8,16},{12,20},{16,24},{20,28},{1,9},{5,13},{9,17},{1... | collective-permute-start | bytes 983048 | tf_op jit(solution)/shard_map/ppermute | solution.py:240
  117.0 19.5 %collective-permute-start.9 = (bf16[640,256]{1,0:T(8,128)(2,1)S(1)}, bf16[640,256]{1,0:T(8,128)(2,1)S(1)}, u32[]{:S(2)}, u32[]{:S(2)}) collective-permute-start(bf16[640,256]{1,0:T(8,128)(2,1)S(1)} %pad_maximum_fusion.37.k0.v0), channel_id=1, source_target_pairs={{0,4},{4,16},{8,12},{12,24},{16,20},{24,28},{1,5},{5,17},{9,13},{1... | collective-permute-start | bytes 983048 | tf_op jit(solution)/shard_map/ppermute | solution.py:240
  235.4 20.3 %collective-permute-start.16 = (bf16[640,256]{1,0:T(8,128)(2,1)S(1)}, bf16[640,256]{1,0:T(8,128)(2,1)S(1)}, u32[]{:S(2)}, u32[]{:S(2)}) collective-permute-start(bf16[640,256]{1,0:T(8,128)(2,1)S(1)} %fusion.115), channel_id=1, source_target_pairs={{8,0},{12,4},{16,8},{20,12},{24,16},{28,20},{9,1},{13,5},{17,9},{2... | collective-permute-start | bytes 983048 | tf_op jit(solution)/shard_map/ppermute | solution.py:240
  280.4 20.4 %collective-permute-start.20 = (bf16[640,256]{1,0:T(8,128)(2,1)S(1)}, bf16[640,256]{1,0:T(8,128)(2,1)S(1)}, u32[]{:S(2)}, u32[]{:S(2)}) collective-permute-start(bf16[640,256]{1,0:T(8,128)(2,1)S(1)} %bitcast.319), channel_id=1, source_target_pairs={{4,0},{12,8},{16,4},{20,16},{24,12},{28,24},{5,1},{13,9},{17,5},{2... | collective-permute-start | bytes 983048 | tf_op jit(solution)/shard_map/ppermute | solution.py:240
  281.9 17.3 %collective-permute-start.18 = (bf16[640,256]{1,0:T(8,128)(2,1)S(1)}, bf16[640,256]{1,0:T(8,128)(2,1)S(1)}, u32[]{:S(2)}, u32[]{:S(2)}) collective-permute-start(bf16[640,256]{1,0:T(8,128)(2,1)S(1)} %bitcast.322), channel_id=1, source_target_pairs={{0,4},{4,0},{8,12},{12,8},{16,20},{20,16},{24,28},{28,24},{1,5},{5... | collective-permute-start | bytes 983048 | tf_op jit(solution)/shard_map/ppermute | solution.py:235
  286.4 29.9 %collective-permute-start.30 = (bf16[512,960]{0,1:T(8,128)(2,1)S(1)}, bf16[512,960]{0,1:T(8,128)(2,1)S(1)}, u32[]{:S(2)}, u32[]{:S(2)}) collective-permute-start(bf16[512,960]{0,1:T(8,128)(2,1)S(1)} %convolution_convert_fusion.4), channel_id=1, source_target_pairs={{0,4},{4,0},{8,12},{12,8},{16,20},{20,16},{24,28},{28,24},{1,5},{5... | collective-permute-start | bytes 2949128 | tf_op jit(solution)/shard_map/ppermute | solution.py:235
  289.0 128.3 %collective-permute-start.39 = (bf16[512,2560]{1,0:T(8,128)(2,1)S(1)}, bf16[512,2560]{1,0:T(8,128)(2,1)S(1)}, u32[]{:S(2)}, u32[]{:S(2)}) collective-permute-start(bf16[512,2560]{1,0:T(8,128)(2,1)S(1)} %convolution_convert_fusion.2), channel_id=1, source_target_pairs={{0,4},{4,0},{8,12},{12,8},{16,20},{20,16},{24,28},{28,24},{1,5},{5... | collective-permute-start | bytes 7864328 | tf_op jit(solution)/shard_map/ppermute | solution.py:235
  317.3 25.8 %collective-permute-start.31 = (bf16[256,960]{0,1:T(8,128)(2,1)S(1)}, bf16[256,960]{0,1:T(8,128)(2,1)S(1)}, u32[]{:S(2)}, u32[]{:S(2)}) collective-permute-start(bf16[256,960]{0,1:T(8,128)(2,1)S(1)} %slice.446), channel_id=1, source_target_pairs={{0,16},{4,20},{8,24},{12,28},{16,0},{20,4},{24,8},{28,12},{1,17},{... | collective-permute-start | bytes 1474568 | tf_op jit(solution)/shard_map/ppermute | solution.py:235
  343.0 70.5 %collective-permute-start.21 = (bf16[512,1603]{0,1:T(8,128)(2,1)S(1)}, bf16[512,1603]{0,1:T(8,128)(2,1)S(1)}, u32[]{:S(2)}, u32[]{:S(2)}) collective-permute-start(bf16[512,1603]{0,1:T(8,128)(2,1)S(1)} %convolution_convert_fusion.3), channel_id=1, source_target_pairs={{0,4},{4,0},{8,12},{12,8},{16,20},{20,16},{24,28},{28,24},{1,5},{5... | collective-permute-start | bytes 4924424 | tf_op jit(solution)/shard_map/ppermute | solution.py:235
  352.0 26.2 %collective-permute-start.35 = (bf16[32,960]{0,1:T(8,128)(2,1)S(1)}, bf16[32,960]{0,1:T(8,128)(2,1)S(1)}, u32[]{:S(2)}, u32[]{:S(2)}) collective-permute-start(bf16[32,960]{0,1:T(8,128)(2,1)S(1)} %get-tuple-element.183), channel_id=1, source_target_pairs={{0,3},{1,0},{2,1},{3,2},{4,7},{5,4},{6,5},{7,6},{8,11},{9,8},{10,9... | collective-permute-start | bytes 184328 | tf_op jit(solution)/shard_map/ppermute | solution.py:344
  358.9 38.0 %collective-permute-start.34 = (bf16[32,960]{0,1:T(8,128)(2,1)S(1)}, bf16[32,960]{0,1:T(8,128)(2,1)S(1)}, u32[]{:S(2)}, u32[]{:S(2)}) collective-permute-start(bf16[32,960]{0,1:T(8,128)(2,1)S(1)} %get-tuple-element.184), channel_id=1, source_target_pairs={{0,2},{1,3},{2,0},{3,1},{4,6},{5,7},{6,4},{7,5},{8,10},{9,11},{10,... | collective-permute-start | bytes 184328 | tf_op jit(solution)/shard_map/ppermute | solution.py:344
  375.5 21.5 %collective-permute-start.33 = (bf16[32,960]{0,1:T(8,128)(2,1)S(1)}, bf16[32,960]{0,1:T(8,128)(2,1)S(1)}, u32[]{:S(2)}, u32[]{:S(2)}) collective-permute-start(bf16[32,960]{0,1:T(8,128)(2,1)S(1)} %get-tuple-element.182), channel_id=1, source_target_pairs={{0,1},{1,2},{2,3},{3,0},{4,5},{5,6},{6,7},{7,4},{8,9},{9,10},{10,1... | collective-permute-start | bytes 184328 | tf_op jit(solution)/shard_map/ppermute | solution.py:344
  378.3 69.7 %collective-permute-start.48 = (bf16[512,2560]{1,0:T(8,128)(2,1)S(1)}, bf16[512,2560]{1,0:T(8,128)(2,1)S(1)}, u32[]{:S(2)}, u32[]{:S(2)}) collective-permute-start(bf16[512,2560]{1,0:T(8,128)(2,1)S(1)} %convolution_convert_fusion.1), channel_id=1, source_target_pairs={{0,4},{4,0},{8,12},{12,8},{16,20},{20,16},{24,28},{28,24},{1,5},{5... | collective-permute-start | bytes 7864328 | tf_op jit(solution)/shard_map/ppermute | solution.py:235
  396.9 40.2 %collective-permute-start.57 = (bf16[2560,512]{1,0:T(8,128)(2,1)S(1)}, bf16[2560,512]{1,0:T(8,128)(2,1)}, u32[]{:S(2)}, u32[]{:S(2)}) collective-permute-start(bf16[2560,512]{1,0:T(8,128)(2,1)S(1)} %convolution_convert_fusion), channel_id=1, source_target_pairs={{0,4},{4,0},{8,12},{12,8},{16,20},{20,16},{24,28},{28,24},{1,5},{5... | collective-permute-start | bytes 7864328 | tf_op jit(solution)/shard_map/ppermute | solution.py:235
  415.2 21.3 %collective-permute-start.22 = (bf16[256,1603]{0,1:T(8,128)(2,1)S(1)}, bf16[256,1603]{0,1:T(8,128)(2,1)S(1)}, u32[]{:S(2)}, u32[]{:S(2)}) collective-permute-start(bf16[256,1603]{0,1:T(8,128)(2,1)S(1)} %slice.433), channel_id=1, source_target_pairs={{0,8},{4,12},{8,0},{12,4},{16,24},{20,28},{24,16},{28,20},{1,9},{5... | collective-permute-start | bytes 2462216 | tf_op jit(solution)/shard_map/ppermute | solution.py:235
  421.2 87.5 %collective-permute-start.40 = (bf16[256,2560]{1,0:T(8,128)(2,1)S(1)}, bf16[256,2560]{1,0:T(8,128)(2,1)S(1)}, u32[]{:S(2)}, u32[]{:S(2)}) collective-permute-start(bf16[256,2560]{1,0:T(8,128)(2,1)S(1)} %slice.456), channel_id=1, source_target_pairs={{0,8},{4,12},{8,0},{12,4},{16,24},{20,28},{24,16},{28,20},{1,9},{5... | collective-permute-start | bytes 3932168 | tf_op jit(solution)/shard_map/ppermute | solution.py:235
  441.1 54.7 %collective-permute-start.58 = (bf16[640,512]{1,0:T(8,128)(2,1)S(1)}, bf16[640,512]{1,0:T(8,128)(2,1)S(1)}, u32[]{:S(2)}, u32[]{:S(2)}) collective-permute-start(bf16[640,512]{1,0:T(8,128)(2,1)S(1)} %dynamic-slice_bitcast_fusion), channel_id=1, source_target_pairs={{0,1},{1,2},{2,3},{3,0},{4,5},{5,6},{6,7},{7,4},{8,9},{9,10},{10,1... | collective-permute-start | bytes 1966088 | tf_op jit(solution)/shard_map/ppermute | solution.py:369
  447.9 19.6 %collective-permute-start.26 = (bf16[32,1603]{0,1:T(8,128)(2,1)S(1)}, bf16[32,1603]{0,1:T(8,128)(2,1)S(1)}, u32[]{:S(2)}, u32[]{:S(2)}) collective-permute-start(bf16[32,1603]{0,1:T(8,128)(2,1)S(1)} %get-tuple-element.168), channel_id=1, source_target_pairs={{0,3},{1,0},{2,1},{3,2},{4,7},{5,4},{6,5},{7,6},{8,11},{9,8},{10,9... | collective-permute-start | bytes 307784 | tf_op jit(solution)/shard_map/ppermute | solution.py:344
  447.9 45.9 %collective-permute-start.25 = (bf16[32,1603]{0,1:T(8,128)(2,1)S(1)}, bf16[32,1603]{0,1:T(8,128)(2,1)S(1)}, u32[]{:S(2)}, u32[]{:S(2)}) collective-permute-start(bf16[32,1603]{0,1:T(8,128)(2,1)S(1)} %get-tuple-element.169), channel_id=1, source_target_pairs={{0,2},{1,3},{2,0},{3,1},{4,6},{5,7},{6,4},{7,5},{8,10},{9,11},{10,... | collective-permute-start | bytes 307784 | tf_op jit(solution)/shard_map/ppermute | solution.py:344
  448.0 45.8 %collective-permute-start.24 = (bf16[32,1603]{0,1:T(8,128)(2,1)S(1)}, bf16[32,1603]{0,1:T(8,128)(2,1)S(1)}, u32[]{:S(2)}, u32[]{:S(2)}) collective-permute-start(bf16[32,1603]{0,1:T(8,128)(2,1)S(1)} %get-tuple-element.167), channel_id=1, source_target_pairs={{0,1},{1,2},{2,3},{3,0},{4,5},{5,6},{6,7},{7,4},{8,9},{9,10},{10,1... | collective-permute-start | bytes 307784 | tf_op jit(solution)/shard_map/ppermute | solution.py:344
  467.4 50.9 %collective-permute-start.49 = (bf16[256,2560]{1,0:T(8,128)(2,1)S(1)}, bf16[256,2560]{1,0:T(8,128)(2,1)S(1)}, u32[]{:S(2)}, u32[]{:S(2)}) collective-permute-start(bf16[256,2560]{1,0:T(8,128)(2,1)S(1)} %slice.466), channel_id=1, source_target_pairs={{0,16},{4,20},{8,24},{12,28},{16,0},{20,4},{24,8},{28,12},{1,17},{... | collective-permute-start | bytes 3932168 | tf_op jit(solution)/shard_map/ppermute | solution.py:235
  496.0 24.2 %collective-permute-start.59 = (bf16[640,512]{1,0:T(8,128)(2,1)S(1)}, bf16[640,512]{1,0:T(8,128)(2,1)S(1)}, u32[]{:S(2)}, u32[]{:S(2)}) collective-permute-start(bf16[640,512]{1,0:T(8,128)(2,1)S(1)} %fusion.57), channel_id=1, source_target_pairs={{0,1},{1,2},{2,3},{3,0},{4,5},{5,6},{6,7},{7,4},{8,9},{9,10},{10,1... | collective-permute-start | bytes 1966088 | tf_op jit(solution)/shard_map/ppermute | solution.py:369
  520.4 19.7 %collective-permute-start.60 = (bf16[640,512]{1,0:T(8,128)(2,1)S(1)}, bf16[640,512]{1,0:T(8,128)(2,1)S(1)}, u32[]{:S(2)}, u32[]{:S(2)}) collective-permute-start(bf16[640,512]{1,0:T(8,128)(2,1)S(1)} %fusion.56), channel_id=1, source_target_pairs={{0,1},{1,2},{2,3},{3,0},{4,5},{5,6},{6,7},{7,4},{8,9},{9,10},{10,1... | collective-permute-start | bytes 1966088 | tf_op jit(solution)/shard_map/ppermute | solution.py:369
  525.4 17.6 %collective-permute-start.44 = (bf16[32,2560]{1,0:T(8,128)(2,1)S(1)}, bf16[32,2560]{1,0:T(8,128)(2,1)S(1)}, u32[]{:S(2)}, u32[]{:S(2)}) collective-permute-start(bf16[32,2560]{1,0:T(8,128)(2,1)S(1)} %get-tuple-element.165), channel_id=1, source_target_pairs={{0,3},{1,0},{2,1},{3,2},{4,7},{5,4},{6,5},{7,6},{8,11},{9,8},{10,9... | collective-permute-start | bytes 491528 | tf_op jit(solution)/shard_map/ppermute | solution.py:344
  527.1 27.1 %collective-permute-start.43 = (bf16[32,2560]{1,0:T(8,128)(2,1)S(1)}, bf16[32,2560]{1,0:T(8,128)(2,1)S(1)}, u32[]{:S(2)}, u32[]{:S(2)}) collective-permute-start(bf16[32,2560]{1,0:T(8,128)(2,1)S(1)} %get-tuple-element.166), channel_id=1, source_target_pairs={{0,2},{1,3},{2,0},{3,1},{4,6},{5,7},{6,4},{7,5},{8,10},{9,11},{10,... | collective-permute-start | bytes 491528 | tf_op jit(solution)/shard_map/ppermute | solution.py:344
  528.5 26.3 %collective-permute-start.42 = (bf16[32,2560]{1,0:T(8,128)(2,1)S(1)}, bf16[32,2560]{1,0:T(8,128)(2,1)S(1)}, u32[]{:S(2)}, u32[]{:S(2)}) collective-permute-start(bf16[32,2560]{1,0:T(8,128)(2,1)S(1)} %get-tuple-element.164), channel_id=1, source_target_pairs={{0,1},{1,2},{2,3},{3,0},{4,5},{5,6},{6,7},{7,4},{8,9},{9,10},{10,1... | collective-permute-start | bytes 491528 | tf_op jit(solution)/shard_map/ppermute | solution.py:344
  536.1 20.6 %collective-permute-start.53 = (bf16[32,2560]{1,0:T(8,128)(2,1)S(1)}, bf16[32,2560]{1,0:T(8,128)(2,1)S(1)}, u32[]{:S(2)}, u32[]{:S(2)}) collective-permute-start(bf16[32,2560]{1,0:T(8,128)(2,1)S(1)} %get-tuple-element.162), channel_id=1, source_target_pairs={{0,3},{1,0},{2,1},{3,2},{4,7},{5,4},{6,5},{7,6},{8,11},{9,8},{10,9... | collective-permute-start | bytes 491528 | tf_op jit(solution)/shard_map/ppermute | solution.py:344
  540.1 27.3 %collective-permute-start.52 = (bf16[32,2560]{1,0:T(8,128)(2,1)S(1)}, bf16[32,2560]{1,0:T(8,128)(2,1)S(1)}, u32[]{:S(2)}, u32[]{:S(2)}) collective-permute-start(bf16[32,2560]{1,0:T(8,128)(2,1)S(1)} %get-tuple-element.163), channel_id=1, source_target_pairs={{0,2},{1,3},{2,0},{3,1},{4,6},{5,7},{6,4},{7,5},{8,10},{9,11},{10,... | collective-permute-start | bytes 491528 | tf_op jit(solution)/shard_map/ppermute | solution.py:344
  543.0 24.5 %collective-permute-start.51 = (bf16[32,2560]{1,0:T(8,128)(2,1)S(1)}, bf16[32,2560]{1,0:T(8,128)(2,1)S(1)}, u32[]{:S(2)}, u32[]{:S(2)}) collective-permute-start(bf16[32,2560]{1,0:T(8,128)(2,1)S(1)} %get-tuple-element.161), channel_id=1, source_target_pairs={{0,1},{1,2},{2,3},{3,0},{4,5},{5,6},{6,7},{7,4},{8,9},{9,10},{10,1... | collective-permute-start | bytes 491528 | tf_op jit(solution)/shard_map/ppermute | solution.py:344
  (234 other events, 1658.2 us)
